TPU v7x, 512 devices: a whole 4x4x16 slice. The times are simulated.
512 devices in a mesh: leaf: 16 (over z), samp: 16 (over y, x), cblk: 2 (over core).
Axes of the slice: x: 4, y: 4, z: 16, core: 2. Of those that a mesh axis runs over, the one named last changes fastest.
Arguments:
- front_matrix: bfloat16 [32768, 32768], P('leaf', ('samp', 'cblk')), may hold values from -0.03125 to 0.03125
- pattern: int32 [32, 32], replicated, may hold values from 0 to 1, as said below
- sample: bfloat16 [256, 32768], P(None, ('samp', 'cblk')), may hold values from -6 to 6
- sketch: float32 [6, 256, 128], replicated, may hold values from -0.375 to 0.375
- level_ranks: int32 [6], replicated, may hold values from 96 to 128, as said below
Outputs:
- leaf_bases: float32 [128, 32768], P(None, ('leaf', 'cblk'))
- path_transfers: float32 [16, 5, 128, 256], P('leaf')
- root_sample: float32 [256, 256], P('samp')
Inputs may be any that keep to these rules, and one draw needn't show every extreme that they name: pattern[a, a] is 1 for every a; other entries are 0 or 1. `level_ranks`: entry l is the rank kept at level l; entry 0 or entry 1 equals 128; entries past the tree's last level with a transfer are not read.
All inputs are finite; a program needn't handle non-finite values.
Results may differ from a plain program's by a relative error of at most 0.0033.
Values may be sent and summed in bfloat16 or wider, within the bound.
No kernel may reach another device: no remote copies, remote signals or barrier semaphores. Data moves between devices by JAX's collectives and lax.ppermute only.
A program may use at most 64 MiB of HBM per device.

v0:
```python
import jax
import jax.numpy as jnp
from jax import lax
from jax.sharding import PartitionSpec as P


def from_partner(shard, axis, bit):
    return lax.ppermute(shard, axis, [(i, i ^ 1 << bit) for i in range(lax.axis_size(axis))])


def compress(columns, level_no, level_ranks, sketch):
    rank_top = sketch.shape[2]
    weights = sketch[level_no]
    share_rows = columns.shape[-2]
    weights = lax.dynamic_slice_in_dim(weights, lax.axis_index("samp") * share_rows, share_rows, 0)
    partial_sum = jnp.einsum("...sm,sk->...km", columns, weights, precision=lax.Precision.HIGHEST)
    projected = lax.psum(partial_sum, "samp")
    kept_mask = (jnp.arange(rank_top) < level_ranks[level_no]).astype(jnp.float32)
    projected = projected * kept_mask[:, None]
    gram_matrix = jnp.einsum(
        "...km,...jm->...kj", projected, projected, precision=lax.Precision.HIGHEST
    ) + jnp.diag(1.0 - kept_mask)
    factor = jnp.linalg.cholesky(gram_matrix)
    level_basis = jax.scipy.linalg.solve_triangular(factor, projected, lower=True)
    reduced = jnp.einsum(
        "...sm,...km->...sk", columns, level_basis, precision=lax.Precision.HIGHEST
    )
    return (level_basis, reduced)


def body(front_matrix, pattern, sample, sketch, level_ranks):
    row_count, column_count = front_matrix.shape
    leaf_rows = row_count // 2
    tree_size = lax.axis_size("leaf")
    tree_depth = tree_size.bit_length() - 1
    my_leaf = lax.axis_index("leaf")
    column_block = lax.axis_index("samp") * lax.axis_size("cblk") + lax.axis_index("cblk")
    rank_top = sketch.shape[2]
    path_slots = sketch.shape[0] - 1
    own_rows = lax.dynamic_slice_in_dim(pattern, 2 * my_leaf, 2, 0)
    per_column = jnp.repeat(own_rows, leaf_rows, axis=1)
    column_mask = lax.dynamic_slice_in_dim(per_column, column_block * column_count, column_count, 1)
    blocked = front_matrix.reshape(2, leaf_rows, column_count)
    masked = (blocked * column_mask.astype(jnp.bfloat16)[:, None, :]).reshape(
        row_count, column_count
    )
    contract_cols = (((1,), (1,)), ((), ()))
    first_part = lax.dot_general(sample, masked, contract_cols, preferred_element_type=jnp.float32)
    first_sample = lax.psum(first_part, ("samp", "cblk")).astype(jnp.bfloat16)
    back_part = jnp.dot(first_sample, masked, preferred_element_type=jnp.float32)
    back_sample = lax.psum(back_part, "leaf").astype(jnp.bfloat16)
    third_part = lax.dot_general(
        back_sample, masked, contract_cols, preferred_element_type=jnp.float32
    )
    sample_part = lax.psum_scatter(third_part, "samp", scatter_dimension=0, tiled=True)
    leaf_columns = lax.psum_scatter(sample_part, "cblk", scatter_dimension=1, tiled=True)
    leaf_basis, reduced = compress(leaf_columns, 0, level_ranks, sketch)
    both_leaves = lax.all_gather(reduced[None], "cblk", axis=0, tiled=True)
    stacked = jnp.concatenate([both_leaves[0], both_leaves[1]], axis=1)
    node_basis, reduced = compress(stacked, 1, level_ranks, sketch)
    path_list = [node_basis]
    for bit_index in range(tree_depth):
        partner = from_partner(reduced, "leaf", bit_index)
        upper_side = my_leaf // 2**bit_index % 2 == 1
        lower_part = jnp.where(upper_side, partner, reduced)
        upper_part = jnp.where(upper_side, reduced, partner)
        stacked = jnp.concatenate([lower_part, upper_part], axis=1)
        if bit_index + 1 < tree_depth:
            node_basis, reduced = compress(stacked, bit_index + 2, level_ranks, sketch)
            path_list.append(node_basis)
    empty = jnp.zeros((rank_top, 2 * rank_top), jnp.float32)
    path_list = path_list + [empty] * (path_slots - len(path_list))
    path_out = jnp.stack(path_list)[None]
    return (leaf_basis, path_out, stacked)


def solution(mesh):
    placed = (P("leaf", ("samp", "cblk")), P(), P(None, ("samp", "cblk")), P(), P())
    return jax.shard_map(
        body,
        mesh=mesh,
        in_specs=placed,
        out_specs=(P(None, ("leaf", "cblk")), P("leaf", None, None, None), P("samp", None)),
        check_vma=False,
    )
```

profile of v0, /device:TPU:1, one launch (start us, length us, event | category | flops | bytes accessed | tf_op | source)
XLA Modules:
  0.0 1104.2 jit_solution(10946651983691231129)
XLA Ops:
  8.3 2.5 bitcast_multiply_fusion
  10.8 1.9 copy-done.1
  12.7 1.3 convolution_bitcast_fusion
  14.0 147.0 %all-reduce.17 = bf16[256,2048]{0,1:T(8,128)(2,1)} all-reduce(f32[256,2048]{0,1:T(8,128)S(1)} %convolution_bitcast_fusion), channel_id=1, replica_groups=mesh['leaf'=16,'samp'=16,'cblk'=2] {'samp','cblk'}, use_global_device_ids=true, to_apply=%region_0.0 | all-reduce | flops 524288 | bytes 3145728 | tf_op jit(solution)/shard_map/psum | solution.py:49
  161.1 3.8 fusion.85
  164.9 61.0 %all-reduce.18 = bf16[256,1024]{1,0:T(8,128)(2,1)S(1)} all-reduce(f32[256,1024]{1,0:T(8,128)S(1)} %fusion.85), channel_id=1, replica_groups=mesh['leaf'=16,'samp'=16,'cblk'=2] {'leaf'}, use_global_device_ids=true, to_apply=%region_1.0 | all-reduce | flops 262144 | bytes 1572864 | tf_op jit(solution)/shard_map/psum | solution.py:51
  225.9 4.9 fusion.86
  230.8 98.0 %reduce-scatter.3.cloned.1.call-done = f32[16,2048]{1,0:T(8,128)} async-done(((f32[256,2048]{1,0:T(8,128)}), f32[16,2048]{1,0:T(8,128)}) %reduce-scatter.3.cloned.1.call-update) | async-done | bytes 131088 | tf_op jit(solution)/shard_map/reduce_scatter | solution.py:55
  329.0 23.2 %reduce-scatter.5.cloned.1.call-done = f32[16,1024]{1,0:T(8,128)} async-done(((f32[16,2048]{1,0:T(8,128)}), f32[16,1024]{1,0:T(8,128)}) %reduce-scatter.5.cloned.1.call-update) | async-done | bytes 65552 | tf_op jit(solution)/shard_map/reduce_scatter | solution.py:56
  352.2 2.2 fusion.61
  356.8 113.5 %all-reduce.8.cloned.1.call-done = f32[128,1024]{1,0:T(8,128)} async-done(((f32[128,1024]{1,0:T(8,128)}), f32[128,1024]{1,0:T(8,128)}) %all-reduce.8.cloned.1.call-update) | async-done | bytes 524304 | tf_op jit(solution)/shard_map/psum | solution.py:17
  470.3 1.9 convolution_add_fusion.4
  472.3 11.7 %cholesky.89 = f32[128,128]{1,0:T(8,128)S(1)} custom-call(f32[128,128]{1,0:T(8,128)S(1)} %fusion.35), custom_call_target="Cholesky" | custom-call | tf_op jit(solution)/shard_map/jit(cholesky)/cholesky | solution.py:23
  485.6 9.8 custom-call.9
  495.5 1.7 fusion.4
  497.2 1.4 fusion.84
  498.6 4.1 all-gather
  502.7 1.0 fusion.56
  505.7 109.3 %all-reduce.10.cloned.1.call-done = f32[128,256]{1,0:T(8,128)} async-done(((f32[128,256]{1,0:T(8,128)}), f32[128,256]{1,0:T(8,128)}) %all-reduce.10.cloned.1.call-update) | async-done | bytes 131088 | tf_op jit(solution)/shard_map/psum | solution.py:17
  615.1 1.3 convolution_add_fusion.3
  616.5 11.7 %cholesky.100 = f32[128,128]{1,0:T(8,128)S(1)} custom-call(f32[128,128]{1,0:T(8,128)S(1)} %fusion.33), custom_call_target="Cholesky" | custom-call | tf_op jit(solution)/shard_map/jit(cholesky)/cholesky | solution.py:23
  629.6 9.8 custom-call.13
  639.4 1.2 bitcast_dynamic-update-slice_fusion.3
  640.8 3.2 collective-permute-start
  644.1 1.2 collective-permute-done
  645.2 1.0 fusion.54
  647.8 113.0 %all-reduce.12.cloned.1.call-done = f32[128,256]{1,0:T(8,128)} async-done(((f32[128,256]{1,0:T(8,128)}), f32[128,256]{1,0:T(8,128)}) %all-reduce.12.cloned.1.call-update) | async-done | bytes 131088 | tf_op jit(solution)/shard_map/psum | solution.py:17
  760.8 1.3 convolution_add_fusion.2
  762.3 11.7 %cholesky.111 = f32[128,128]{1,0:T(8,128)S(1)} custom-call(f32[128,128]{1,0:T(8,128)S(1)} %fusion.31), custom_call_target="Cholesky" | custom-call | tf_op jit(solution)/shard_map/jit(cholesky)/cholesky | solution.py:23
  775.3 9.8 custom-call.14
  785.1 1.2 bitcast_dynamic-update-slice_fusion.2
  786.6 4.2 collective-permute-start.1
  790.8 1.1 collective-permute-done.1
  791.9 1.0 fusion.52
  794.3 113.2 %all-reduce.14.cloned.1.call-done = f32[128,256]{1,0:T(8,128)} async-done(((f32[128,256]{1,0:T(8,128)}), f32[128,256]{1,0:T(8,128)}) %all-reduce.14.cloned.1.call-update) | async-done | bytes 131088 | tf_op jit(solution)/shard_map/psum | solution.py:17
  907.5 1.3 convolution_add_fusion.1
  908.9 11.7 %cholesky.122 = f32[128,128]{1,0:T(8,128)S(1)} custom-call(f32[128,128]{1,0:T(8,128)S(1)} %fusion.29), custom_call_target="Cholesky" | custom-call | tf_op jit(solution)/shard_map/jit(cholesky)/cholesky | solution.py:23
  922.0 9.8 custom-call.15
  931.8 1.2 bitcast_dynamic-update-slice_fusion.1
  933.2 7.7 collective-permute-start.2
  941.7 1.0 fusion.50
  944.0 113.1 %all-reduce.16.cloned.1.call-done = f32[128,256]{1,0:T(8,128)} async-done(((f32[128,256]{1,0:T(8,128)}), f32[128,256]{1,0:T(8,128)}) %all-reduce.16.cloned.1.call-update) | async-done | bytes 131088 | tf_op jit(solution)/shard_map/psum | solution.py:17
  1057.2 1.3 convolution_add_fusion
  1058.6 11.7 %cholesky.133 = f32[128,128]{1,0:T(8,128)S(1)} custom-call(f32[128,128]{1,0:T(8,128)S(1)} %fusion.27), custom_call_target="Cholesky" | custom-call | tf_op jit(solution)/shard_map/jit(cholesky)/cholesky | solution.py:23
  1071.7 9.8 custom-call.16
  1081.5 1.2 bitcast_dynamic-update-slice_fusion
  1082.9 12.6 %collective-permute-start.3 = (f32[16,128]{1,0:T(8,128)S(1)}, f32[16,128]{1,0:T(8,128)S(1)}, u32[]{:S(2)}, u32[]{:S(2)}) collective-permute-start(f32[16,128]{1,0:T(8,128)S(1)} %fusion.49), channel_id=1, source_target_pairs={{0,256},{32,288},{64,320},{96,352},{128,384},{160,416},{192,448},{... | collective-permute-start | bytes 24584 | tf_op jit(solution)/shard_map/ppermute | solution.py:8
  1095.5 1.0 collective-permute-done.3
  (80 shorter events, 19.4 us)
Async XLA Ops:
  7.2 5.5 copy-start
  7.2 321.7 %reduce-scatter.3.cloned.1.call-start = ((), (), s32[]{:S(2)}) async-start(), calls=%async_computation.2 | async-start | bytes 2228224 | tf_op jit(solution)/shard_map/reduce_scatter | solution.py:55
  10.8 1.9 copy-start.1
  225.9 103.1 %copy-start.3 = (f32[6,256,128]{2,1,0:T(8,128)S(1)}, f32[6,256,128]{2,1,0:T(8,128)}, u32[]{:S(2)}) copy-start(f32[6,256,128]{2,1,0:T(8,128)} %param.11) | copy-start | bytes 2359300
  225.9 129.0 %copy-start.5 = (s32[6]{0:T(128)S(1)}, s32[6]{0:T(128)}, u32[]{:S(2)}) copy-start(s32[6]{0:T(128)} %param.12) | copy-start | bytes 76
  230.8 121.4 %reduce-scatter.5.cloned.1.call-start = ((), (), s32[]{:S(2)}) async-start(), calls=%async_computation.3 | async-start | bytes 196608 | tf_op jit(solution)/shard_map/reduce_scatter | solution.py:56
  328.9 141.4 %all-reduce.8.cloned.1.call-start = ((), (), s32[]{:S(2)}) async-start(), calls=%async_computation.4 | async-start | bytes 1048576 | tf_op jit(solution)/shard_map/psum | solution.py:17
  354.5 260.6 %all-reduce.10.cloned.1.call-start = ((), (), s32[]{:S(2)}) async-start(), calls=%async_computation.5 | async-start | bytes 262144 | tf_op jit(solution)/shard_map/psum | solution.py:17
  497.2 600.0 %copy-start.2 = (f32[128,1024]{1,0:T(8,128)}, f32[128,1024]{1,0:T(8,128)S(1)}, u32[]{:S(2)}) copy-start(f32[128,1024]{1,0:T(8,128)S(1)} %fusion.4) | copy-start | bytes 1572868
  503.7 257.1 %all-reduce.12.cloned.1.call-start = ((), (), s32[]{:S(2)}) async-start(), calls=%async_computation.6 | async-start | bytes 262144 | tf_op jit(solution)/shard_map/psum | solution.py:17
  640.8 4.4 collective-permute-start
  646.2 261.3 %all-reduce.14.cloned.1.call-start = ((), (), s32[]{:S(2)}) async-start(), calls=%async_computation.7 | async-start | bytes 262144 | tf_op jit(solution)/shard_map/psum | solution.py:17
  786.6 5.3 collective-permute-start.1
  792.9 264.3 %all-reduce.16.cloned.1.call-start = ((), (), s32[]{:S(2)}) async-start(), calls=%async_computation.8 | async-start | bytes 262144 | tf_op jit(solution)/shard_map/psum | solution.py:17
  933.2 8.4 collective-permute-start.2
  1082.9 13.6 %collective-permute-start.3 = (f32[16,128]{1,0:T(8,128)S(1)}, f32[16,128]{1,0:T(8,128)S(1)}, u32[]{:S(2)}, u32[]{:S(2)}) collective-permute-start(f32[16,128]{1,0:T(8,128)S(1)} %fusion.49), channel_id=1, source_target_pairs={{0,256},{32,288},{64,320},{96,352},{128,384},{160,416},{192,448},{... | collective-permute-start | bytes 24584 | tf_op jit(solution)/shard_map/ppermute | solution.py:8
  1095.5 1.6 copy-start.4
Sparse Core Ops, SparseCore 0:
  230.9 97.8 reduce-scatter.2
  331.6 20.5 reduce-scatter.4
  356.0 114.2 all-reduce.7
  503.8 111.1 all-reduce.9
  646.4 114.4 all-reduce.11
  793.0 114.4 all-reduce.13
  942.8 114.3 all-reduce.15
where the time goes:
time: 1110 us; the launch traced here: 1100 us
  waiting for transfers between devices  687 us (62%)
  blocking collectives  212 us (19%)
  other arithmetic  124 us (11%)
  matrix products  32.1 us (3%)
  starting transfers between devices  29.3 us (3%)
  between operations  15 us (1%)
    psum x5, waiting for transfers between devices, compress(): projected = lax.psum(partial_sum, 'samp')  562 us
    psum x1, blocking collectives, body(): first_sample = lax.psum(first_part, ('samp', 'cblk')).astype(jnp.bfloat16)  147 us
    reduce_scatter x1, waiting for transfers between devices, body(): lax.psum_scatter(third_part, 'samp', scatter_dimension=0, tiled=True)  98 us
    another operation x15, other arithmetic, compress(): factor = jnp.linalg.cholesky(gram_matrix)  62 us
    psum x1, blocking collectives, body(): back_sample = lax.psum(back_part, 'leaf').astype(jnp.bfloat16)  61 us
    another operation x10, other arithmetic, compress(): jax.scipy.linalg.solve_triangular(factor, projected, lower=True)  52.3 us
    ppermute x4, starting transfers between devices, from_partner(): lax.ppermute(shard, axis, [(i, i ^ 1 << bit) for i in range(lax.axis_size...  27.7 us
    reduce_scatter x1, waiting for transfers between devices, body(): lax.psum_scatter(sample_part, 'cblk', scatter_dimension=1, tiled=True)  23.2 us
  transfers between devices with their start and end apart: 11, of which 11 were waited for; matrix products, arithmetic and copies ran while one was open for 1% of the time, Pallas kernels for 0%

commit v1 on v0

v1 whole, which is shorter than its diff:
```python
import jax
import jax.numpy as jnp
from jax import lax
from jax.experimental import pallas as pl
from jax.experimental.pallas import tpu as pltpu
from jax.sharding import PartitionSpec as P

HIGHEST = lax.Precision.HIGHEST
COLS = (((1,), (1,)), ((), ()))
ROWS = (((0,), (0,)), ((), ()))
ROW_BLOCK = 8


def exact_dot(a, b, dims):
    return lax.dot_general(a, b, dims, precision=HIGHEST, preferred_element_type=jnp.float32)


def inverse_factor(gram):
    n = gram.shape[0]
    count = n // ROW_BLOCK
    lane = lax.broadcasted_iota(jnp.int32, (ROW_BLOCK, n), 1)
    row = lax.broadcasted_iota(jnp.int32, (ROW_BLOCK, n), 0)
    panels = [gram[ROW_BLOCK * i : ROW_BLOCK * (i + 1), :] for i in range(count)]
    finished = []
    for b in range(count):
        panel = panels[b]
        start = ROW_BLOCK * b
        stop = start + ROW_BLOCK
        columns = [
            jnp.broadcast_to(panel[:, start + j : start + j + 1], (ROW_BLOCK, n))
            for j in range(ROW_BLOCK)
        ]
        root = jnp.zeros((ROW_BLOCK, n), jnp.float32)
        inverse = jnp.zeros((ROW_BLOCK, n), jnp.float32)
        for k in range(ROW_BLOCK):
            pivot = jnp.broadcast_to(columns[k][k : k + 1, :], (ROW_BLOCK, n))
            over = 1.0 / pivot
            factor = jnp.where(row > k, columns[k] * over, 0.0)
            here = lane == start + k
            pivot_row = jnp.where(here, 1.0, jnp.broadcast_to(panel[k : k + 1, :], (ROW_BLOCK, n)))
            panel = jnp.where(here & (row >= k), jnp.where(row == k, 1.0, 0.0), panel)
            panel = panel - factor * pivot_row
            for j in range(k + 1, ROW_BLOCK):
                columns[j] = columns[j] - factor * jnp.broadcast_to(
                    columns[j][k : k + 1, :], (ROW_BLOCK, n)
                )
            inverse = jnp.where(row == k, over, inverse)
            root = jnp.where(row == k, lax.rsqrt(pivot), root)
        panel = jnp.where((lane <= start + row) | (lane >= stop), panel, 0.0)
        finished.append(panel * jnp.where(lane < stop, root, 0.0))
        if b + 1 < count:
            scaled = panel * inverse
            outside = (lane < start) | (lane >= stop)
            update = exact_dot(scaled[:, stop : stop + ROW_BLOCK], panel, ROWS)
            panels[b + 1] = jnp.where(outside, panels[b + 1], 0.0) - update
            if b + 2 < count:
                update = exact_dot(scaled[:, stop + ROW_BLOCK :], panel, ROWS)
                for i in range(b + 2, count):
                    at = ROW_BLOCK * (i - b - 2)
                    panels[i] = jnp.where(outside, panels[i], 0.0) - update[at : at + ROW_BLOCK, :]
    return jnp.concatenate(finished, axis=0)


def compress_values(parts, weights, rank):
    top = weights.shape[1]
    keep = (lax.broadcasted_iota(jnp.int32, (top, 1), 0) < rank).astype(jnp.float32)
    views = [exact_dot(weights, part, ROWS) * keep for part in parts]
    gram = sum(exact_dot(view, view, COLS) for view in views)
    at_row = lax.broadcasted_iota(jnp.int32, (top, top), 0)
    at_col = lax.broadcasted_iota(jnp.int32, (top, top), 1)
    gram = gram + jnp.where((at_row == at_col) & (at_row >= rank), 1.0, 0.0)
    cross = sum(exact_dot(part, view, COLS) for part, view in zip(parts, views, strict=True))
    inverse = inverse_factor(gram)
    bases = [exact_dot(inverse, view, (((1,), (0,)), ((), ()))) for view in views]
    return bases, exact_dot(cross, inverse, COLS)


def leaf_kernel(rank_ref, columns_ref, weights_ref, basis_ref, reduced_ref):
    bases, reduced = compress_values([columns_ref[...]], weights_ref[...], rank_ref[0])
    basis_ref[...] = bases[0]
    reduced_ref[...] = reduced


def node_kernel(rank_ref, mine_ref, other_ref, weights_ref, basis_ref, reduced_ref):
    upper = rank_ref[1] == 1
    mine = mine_ref[...]
    other = other_ref[...]
    parts = [jnp.where(upper, other, mine), jnp.where(upper, mine, other)]
    bases, reduced = compress_values(parts, weights_ref[...], rank_ref[0])
    top = weights_ref.shape[1]
    basis_ref[:, :top] = bases[0]
    basis_ref[:, top:] = bases[1]
    reduced_ref[...] = reduced


def compress(scalars, parts, weights):
    samples, top = weights.shape
    width = sum(part.shape[1] for part in parts)
    kernel = leaf_kernel if len(parts) == 1 else node_kernel
    vmem = pl.BlockSpec(memory_space=pltpu.VMEM)
    return pl.pallas_call(
        kernel,
        in_specs=[pl.BlockSpec(memory_space=pltpu.SMEM)] + [vmem] * (len(parts) + 1),
        out_specs=(vmem, vmem),
        out_shape=(
            jax.ShapeDtypeStruct((top, width), jnp.float32),
            jax.ShapeDtypeStruct((samples, top), jnp.float32),
        ),
        name="compress_leaf" if len(parts) == 1 else "compress_node",
    )(scalars, *parts, weights)


def swap_cores(x):
    return lax.ppermute(x, "cblk", [(0, 1), (1, 0)])


def exchange(x, axis, groups=None):
    return lax.all_to_all(x, axis, 0, 0, axis_index_groups=groups)


def spread(x, count, axis, groups=None):
    return exchange(jnp.broadcast_to(x[None], (count,) + x.shape), axis, groups)


def body(front, pattern, sample, sketch, level_ranks):
    rows, width = front.shape
    leaf_rows = rows // 2
    samples = sample.shape[0]
    half = samples // 2
    top = sketch.shape[2]
    n_leaf = lax.axis_size("leaf")
    n_samp = lax.axis_size("samp")
    depth = n_leaf.bit_length() - 1
    z = lax.axis_index("leaf")
    s = lax.axis_index("samp")
    c = lax.axis_index("cblk")
    f32 = jnp.float32
    bf16 = jnp.bfloat16

    block = 2 * s + c
    flags = lax.dynamic_slice(pattern, (2 * z, block), (2, 1))
    leaf_mask = jnp.repeat(flags, leaf_rows, axis=0).reshape(1, rows)

    def first_half(which):
        part = lax.dynamic_slice_in_dim(sample, which * half, half, 0)
        return lax.dot_general(part, front, COLS, preferred_element_type=f32)

    away = swap_cores(first_half(1 - c) * leaf_mask.astype(f32))
    total = first_half(c) * leaf_mask.astype(f32) + away
    pieces = exchange(total.reshape(n_samp, half // n_samp, rows), "samp")
    piece = jnp.sum(pieces, axis=0).astype(bf16)
    mine = spread(piece, n_samp, "samp").reshape(half, rows)
    other = swap_cores(mine)
    first_sample = jnp.where(
        c == 0, jnp.concatenate([mine, other], 0), jnp.concatenate([other, mine], 0)
    )
    first_sample = first_sample * leaf_mask.astype(bf16)

    back_part = jnp.dot(first_sample, front, preferred_element_type=f32)
    odd = z % 2
    pairs = []
    for i in range(n_leaf):
        pairs.append((2 * i, 2 * (i ^ 1)))
        pairs.append((2 * i + 1, 2 * ((i + 1 if i % 2 else i - 1) % n_leaf) + 1))
    group = n_leaf // 2
    parity = [list(range(p, n_leaf, 2)) for p in range(2)]
    given = lax.dynamic_slice_in_dim(back_part, (1 - odd) * half, half, 0)
    kept = lax.dynamic_slice_in_dim(back_part, odd * half, half, 0)
    kept = kept + lax.ppermute(given, ("leaf", "cblk"), pairs)
    pieces = exchange(kept.reshape(group, half // group, width), "leaf", parity)
    piece = jnp.sum(pieces, axis=0).astype(bf16)
    mine = spread(piece, group, "leaf", parity).reshape(half, width)
    other = lax.ppermute(mine, ("leaf", "cblk"), pairs)
    back_sample = jnp.where(
        odd == 0, jnp.concatenate([mine, other], 0), jnp.concatenate([other, mine], 0)
    )

    def third_half(which):
        part = lax.dynamic_slice_in_dim(front, which * leaf_rows, leaf_rows, 0)
        flag = lax.dynamic_slice_in_dim(flags, which, 1, 0).astype(f32)
        return lax.dot_general(back_sample, part, COLS, preferred_element_type=f32) * flag

    away = swap_cores(third_half(1 - c))
    total = third_half(c) + away
    pieces = exchange(total.reshape(n_samp, samples // n_samp, leaf_rows), "samp")
    piece = jnp.sum(pieces, axis=0)
    leaf_columns = spread(piece, n_samp, "samp").reshape(samples, leaf_rows)

    def scalars(level, upper):
        return jnp.stack([level_ranks[level], upper.astype(jnp.int32)])

    leaf_basis, reduced = compress(scalars(0, c), [leaf_columns], sketch[0])
    path = []
    node_basis, reduced = compress(scalars(1, c), [reduced, swap_cores(reduced)], sketch[1])
    path.append(node_basis)
    for bit in range(depth - 1):
        partner = lax.ppermute(reduced, "leaf", [(i, i ^ (1 << bit)) for i in range(n_leaf)])
        node_basis, reduced = compress(
            scalars(bit + 2, z // 2**bit % 2), [reduced, partner], sketch[bit + 2]
        )
        path.append(node_basis)
    share = samples // n_samp
    mine = lax.dynamic_slice_in_dim(reduced, s * share, share, 0)
    bit = depth - 1
    other = lax.ppermute(mine, "leaf", [(i, i ^ (1 << bit)) for i in range(n_leaf)])
    upper = z // 2**bit % 2 == 1
    root = jnp.concatenate([jnp.where(upper, other, mine), jnp.where(upper, mine, other)], axis=1)
    empty = jnp.zeros((top, 2 * top), f32)
    path = path + [empty] * (sketch.shape[0] - 1 - len(path))
    return (leaf_basis, jnp.stack(path)[None], root)


def solution(mesh):
    placed = (P("leaf", ("samp", "cblk")), P(), P(None, ("samp", "cblk")), P(), P())
    return jax.shard_map(
        body,
        mesh=mesh,
        in_specs=placed,
        out_specs=(P(None, ("leaf", "cblk")), P("leaf", None, None, None), P("samp", None)),
        check_vma=False,
    )
```

time: 1110 us -> 310 us (0.28)
  waiting for transfers between devices: 687 us -> 60.6 us
  other arithmetic: 124 us -> 8.42 us
  blocking collectives: 212 us -> 113 us
  Pallas kernels: 0 us -> 42.1 us
  starting transfers between devices: 29.3 us -> 47.7 us
  matrix products: 32.1 us -> 15.5 us
  local copies, waits for them, and re-layouts: 4.32 us -> 19.5 us
  between operations: 15 us -> 2.29 us
    psum x5 -> x0, waiting for transfers between devices: 562 us -> none  [compress(): projected = lax.psum(partial_sum, 'samp')]
    psum x2 -> x0, blocking collectives: 208 us -> none  [the longest x1 147 us: body(): first_sample = lax.psum(first_part, ('samp', 'cblk')).astype(jnp.bfloat16)]
    reduce_scatter x2 -> x0, waiting for transfers between devices: 121 us -> none  [the longest x1 98 us: body(): lax.psum_scatter(third_part, 'samp', scatter_dimension=0, tiled=True)]
    all_to_all x0 -> x5, blocking collectives: none -> 113 us  [exchange(): return lax.all_to_all(x, axis, 0, 0, axis_index_groups=groups)]
    another operation x25 -> x5, other arithmetic: 114 us -> 5.78 us  [scalars(): return jnp.stack([level_ranks[level], upper.astype(jnp.int32)])]
    ppermute x4 -> x10, waiting for transfers between devices: 4 us -> 50.6 us  [the longest x3 26.3 us: body(): lax.ppermute(reduced, 'leaf', [(i, i ^ 1 << bit) for i in range(n_leaf)])]
    pallas_call x0 -> x4, Pallas kernels: none -> 42.1 us  [compress(): pl.pallas_call(kernel, in_specs=[pl.BlockSpec(memory_space=pltpu.SMEM)] +...]
    ppermute x4 -> x10, starting transfers between devices: 27.7 us -> 44 us  [the longest x4 22.4 us: swap_cores(): return lax.ppermute(x, 'cblk', [(0, 1), (1, 0)])]
  transfers between devices with their start and end apart: 11 -> 11, of which waited for: 11 -> 10; matrix products, arithmetic and copies ran while one was open for 1% -> 4% of each run, Pallas kernels for 0% -> 0%
where the time goes in v1:
time: 310 us; the launch traced here: 309 us
  blocking collectives  113 us (36%)
  waiting for transfers between devices  60.6 us (20%)
  starting transfers between devices  47.7 us (15%)
  Pallas kernels  42.1 us (14%)
  local copies, waits for them, and re-layouts  19.5 us (6%)
  matrix products  15.5 us (5%)
  other arithmetic  8.42 us (3%)
    all_to_all x5, blocking collectives, exchange(): return lax.all_to_all(x, axis, 0, 0, axis_index_groups=groups)  113 us
    pallas_call x4, Pallas kernels, compress(): pl.pallas_call(kernel, in_specs=[pl.BlockSpec(memory_space=pltpu.SMEM)] +...  42.1 us
    ppermute x3, waiting for transfers between devices, body(): lax.ppermute(reduced, 'leaf', [(i, i ^ 1 << bit) for i in range(n_leaf)])  26.3 us
    ppermute x4, starting transfers between devices, swap_cores(): return lax.ppermute(x, 'cblk', [(0, 1), (1, 0)])  22.4 us
    all_to_all x1, waiting for transfers between devices, exchange(): return lax.all_to_all(x, axis, 0, 0, axis_index_groups=groups)  9.97 us
    ppermute x1, starting transfers between devices, body(): kept = kept + lax.ppermute(given, ('leaf', 'cblk'), pairs)  9.72 us
    pallas_call x1, local copies, waits for them, and re-layouts, compress(): pl.pallas_call(kernel, in_specs=[pl.BlockSpec(memory_space=pltpu.SMEM)] +...  9.52 us
    ppermute x1, waiting for transfers between devices, body(): lax.ppermute(mine, 'leaf', [(i, i ^ 1 << bit) for i in range(n_leaf)])  8.96 us
  transfers between devices with their start and end apart: 11, of which 10 were waited for; matrix products, arithmetic and copies ran while one was open for 4% of the time, Pallas kernels for 0%

profile of v1, /device:TPU:1, one launch (start us, length us, event | category | flops | bytes accessed | tf_op | source)
XLA Modules:
  0.0 308.6 jit_solution(9123499386803019710)
XLA Ops:
  0.7 0.9 convert_reduce_fusion
  1.7 3.7 %convolution_multiply_fusion = f32[128,2048]{1,0:T(8,128)S(1)} fusion(bf16[2048,1024]{1,0:T(8,128)(2,1)} %param.5, f32[2048]{0:T(1024)S(1)} %bitcast.53, bf16[256,1024]{1,0:T(8,128)(2,1)S(1)} %copy-done, s32[]{:T(128)S(6)} %select_n.107), kind=kOutput, calls=%fused_computation | convolution fusion | flops 537133056 | bytes 5513220 | tf_op jit(solution)/shard_map/dot_general | solution.py:146
  5.4 8.7 %collective-permute-start = (f32[128,2048]{1,0:T(8,128)S(1)}, f32[128,2048]{1,0:T(8,128)S(1)}, u32[]{:S(2)}, u32[]{:S(2)}) collective-permute-start(f32[128,2048]{1,0:T(8,128)S(1)} %convolution_multiply_fusion), channel_id=1, source_target_pairs={{0,1},{1,0},{2,3},{3,2},{4,5},{5,4},{6,7},{7,6},{8,9},{9,8},{10,11... | collective-permute-start | bytes 3145736 | tf_op jit(solution)/shard_map/ppermute | solution.py:114
  14.2 2.3 collective-permute-done
  16.4 3.7 %fusion.1 = f32[16,8,2048]{2,1,0:T(8,128)S(1)} fusion(f32[128,2048]{1,0:T(8,128)S(1)} %collective-permute-done, bf16[2048,1024]{1,0:T(8,128)(2,1)} %param.5, f32[2048]{0:T(1024)S(1)} %bitcast.54, bf16[256,1024]{1,0:T(8,128)(2,1)S(1)} %copy-done, s32[]{:T(128)S(6)} %select_n.104), kind=kOutput, calls=%fused_computation.3 | convolution fusion | flops 537395200 | bytes 6561796 | tf_op jit(solution)/shard_map/dot_general | solution.py:146
  20.1 19.3 %all_to_all.30 = f32[16,8,2048]{2,1,0:T(8,128)S(1)} all-to-all(f32[16,8,2048]{2,1,0:T(8,128)S(1)} %fusion.1), channel_id=1, replica_groups=mesh['leaf'=16,'samp'=16,'cblk'=2] {'samp'}, dimensions={0} | all-to-all | bytes 2097152 | tf_op jit(solution)/shard_map/all_to_all | solution.py:118
  39.5 13.3 %all_to_all.31 = bf16[16,8,2048]{2,1,0:T(8,128)(2,1)S(1)} all-to-all(bf16[16,8,2048]{2,1,0:T(8,128)(2,1)S(1)} %broadcast_in_dim.13), channel_id=1, replica_groups=mesh['leaf'=16,'samp'=16,'cblk'=2] {'samp'}, dimensions={0} | all-to-all | bytes 1048576 | tf_op jit(solution)/shard_map/all_to_all | solution.py:118
  52.8 4.0 %collective-permute-start.1 = (bf16[128,2048]{1,0:T(8,128)(2,1)S(1)}, bf16[128,2048]{1,0:T(8,128)(2,1)S(1)}, u32[]{:S(2)}, u32[]{:S(2)}) collective-permute-start(bf16[128,2048]{1,0:T(8,128)(2,1)S(1)} %bitcast.48), channel_id=1, source_target_pairs={{0,1},{1,0},{2,3},{3,2},{4,5},{5,4},{6,7},{7,6},{8,9},{9,8},{10,11... | collective-permute-start | bytes 1572872 | tf_op jit(solution)/shard_map/ppermute | solution.py:114
  56.9 0.9 convert_reduce_fusion.1
  58.4 3.5 %fusion.16 = f32[256,1024]{1,0:T(8,128)S(1)} fusion(bf16[2048,1024]{1,0:T(8,128)(2,1)} %param.5, bf16[128,2048]{1,0:T(8,128)(2,1)S(1)} %collective-permute-done.1, bf16[128,2048]{1,0:T(8,128)(2,1)S(1)} %bitcast.49, pred[]{:T(512)S(6)} %eq.16, bf16[2048]{0:T(1024)(128)(2,1)S(1)} %bitcast.56), kind=kOutput, calls=%fused_computation.13 | convolution fusion | flops 1080557568 | bytes 6295553 | tf_op jit(solution)/shard_map/dot_general | solution.py:159
  61.9 9.7 %collective-permute-start.2 = (f32[128,1024]{1,0:T(8,128)S(1)}, f32[128,1024]{1,0:T(8,128)S(1)}, u32[]{:S(2)}, u32[]{:S(2)}) collective-permute-start(f32[128,1024]{1,0:T(8,128)S(1)} %constant_dynamic-slice_fusion.1), channel_id=1, source_target_pairs={{0,32},{1,481},{32,0},{33,65},{64,96},{65,33},{96,64},{97,129},{12... | collective-permute-start | bytes 1572872 | tf_op jit(solution)/shard_map/ppermute | solution.py:169
  71.6 6.5 %collective-permute-done.2 = f32[128,1024]{1,0:T(8,128)S(1)} collective-permute-done((f32[128,1024]{1,0:T(8,128)S(1)}, f32[128,1024]{1,0:T(8,128)S(1)}, u32[]{:S(2)}, u32[]{:S(2)}) %collective-permute-start.2) | collective-permute-done | bytes 524320 | tf_op jit(solution)/shard_map/ppermute | solution.py:169
  78.2 39.5 %all_to_all.32 = f32[8,16,1024]{2,1,0:T(8,128)S(1)} all-to-all(f32[8,16,1024]{2,1,0:T(8,128)S(1)} %bitcast.46), channel_id=1, replica_groups={{0,64,128,192,256,320,384,448},{32,96,160,224,288,352,416,480},{1,65,12..., dimensions={0} | all-to-all | bytes 1048576 | tf_op jit(solution)/shard_map/all_to_all | solution.py:118
  117.8 21.3 %all_to_all.33 = bf16[8,16,1024]{2,1,0:T(8,128)(2,1)S(1)} all-to-all(bf16[8,16,1024]{2,1,0:T(8,128)(2,1)S(1)} %broadcast_in_dim.29), channel_id=1, replica_groups={{0,64,128,192,256,320,384,448},{32,96,160,224,288,352,416,480},{1,65,12..., dimensions={0} | all-to-all | bytes 524288 | tf_op jit(solution)/shard_map/all_to_all | solution.py:118
  139.1 1.9 collective-permute-start.3
  141.1 1.4 fusion.37
  143.1 4.4 %collective-permute-done.3 = bf16[128,1024]{1,0:T(8,128)(2,1)S(1)} collective-permute-done((bf16[128,1024]{1,0:T(8,128)(2,1)S(1)}, bf16[128,1024]{1,0:T(8,128)(2,1)S(1)}, u32[]{:S(2)}, u32[]{:S(2)}) %collective-permute-start.3) | collective-permute-done | bytes 262176 | tf_op jit(solution)/shard_map/ppermute | solution.py:173
  147.4 2.3 fusion.12
  149.8 4.4 %collective-permute-start.4 = (f32[256,1024]{1,0:T(8,128)S(1)}, f32[256,1024]{1,0:T(8,128)S(1)}, u32[]{:S(2)}, u32[]{:S(2)}) collective-permute-start(f32[256,1024]{1,0:T(8,128)S(1)} %fusion.12), channel_id=1, source_target_pairs={{0,1},{1,0},{2,3},{3,2},{4,5},{5,4},{6,7},{7,6},{8,9},{9,8},{10,11... | collective-permute-start | bytes 3145736 | tf_op jit(solution)/shard_map/ppermute | solution.py:114
  154.8 1.6 collective-permute-done.4
  156.4 2.3 fusion.9
  158.8 19.1 %all_to_all.34 = f32[16,16,1024]{2,1,0:T(8,128)S(1)} all-to-all(f32[16,16,1024]{2,1,0:T(8,128)S(1)} %bitcast.47), channel_id=1, replica_groups=mesh['leaf'=16,'samp'=16,'cblk'=2] {'samp'}, dimensions={0} | all-to-all | bytes 2097152 | tf_op jit(solution)/shard_map/all_to_all | solution.py:118
  178.0 1.1 broadcast_in_dim.30
  179.1 3.7 %all-to-all-start.5 = ((f32[16,16,1024]{2,1,0:T(8,128)}), f32[16,16,1024]{2,1,0:T(8,128)S(1)}, u32[]{:S(2)}, u32[]{:S(2)}) async-start(f32[16,16,1024]{2,1,0:T(8,128)} %broadcast_in_dim.30), calls=%async_computation.5 | async-start | bytes 2097152 | tf_op jit(solution)/shard_map/all_to_all | solution.py:118
  183.5 1.3 pad_add_fusion.rank_ref
  184.7 1.2 pad_add_fusion.1.rank_ref
  186.0 1.2 pad_add_fusion.2.rank_ref
  187.2 0.8 slice_bitcast_fusion
  188.0 10.0 %all-to-all-done.5 = f32[16,16,1024]{2,1,0:T(8,128)S(1)} async-done(((f32[16,16,1024]{2,1,0:T(8,128)}), f32[16,16,1024]{2,1,0:T(8,128)S(1)}, u32[]{:S(2)}, u32[]{:S(2)}) %all-to-all-start.5) | async-done | bytes 1048608 | tf_op jit(solution)/shard_map/all_to_all | solution.py:118
  198.0 1.0 copy-done.1
  199.0 11.2 %compress_leaf.1 = (f32[128,1024]{1,0:T(8,128)}, f32[256,128]{1,0:T(8,128)}) custom-call(s32[2]{0:T(128)} %pad_add_fusion.rank_ref, f32[256,1024]{1,0:T(8,128)} %bitcast.45, f32[256,128]{1,0:T(8,128)} %get-tuple-element.30.weights_ref), custom_call_target="tpu_custom_call" | custom-call | tf_op jit(solution)/shard_map/compress_leaf/pallas_call | solution.py:101
  210.2 5.2 %collective-permute-start.5 = (f32[256,128]{1,0:T(8,128)}, f32[256,128]{1,0:T(8,128)S(1)}, u32[]{:S(2)}, u32[]{:S(2)}) collective-permute-start(f32[256,128]{1,0:T(8,128)} %get-tuple-element.14.mine_ref), channel_id=1, source_target_pairs={{0,1},{1,0},{2,3},{3,2},{4,5},{5,4},{6,7},{7,6},{8,9},{9,8},{10,11... | collective-permute-start | bytes 393224 | tf_op jit(solution)/shard_map/ppermute | solution.py:114
  215.4 1.3 pad_add_fusion.3.rank_ref
  218.1 10.3 %compress_node.4 = (f32[128,256]{1,0:T(8,128)}, f32[256,128]{1,0:T(8,128)}) custom-call(s32[2]{0:T(128)} %pad_add_fusion.1.rank_ref, f32[256,128]{1,0:T(8,128)} %get-tuple-element.14.mine_ref, f32[256,128]{1,0:T(8,128)} %copy-done.3, f32[256,128]{1,0:T(8,128)} %get-tuple-element.29.weights_ref), custom_call_target="tpu_custom_call" | custom-call | tf_op jit(solution)/shard_map/compress_node/pallas_call | solution.py:101
  228.4 1.9 collective-permute-start.6
  230.3 0.9 bitcast_dynamic-update-slice_fusion.3
  231.2 4.3 %collective-permute-done.6.other_ref = f32[256,128]{1,0:T(8,128)S(1)} collective-permute-done((f32[256,128]{1,0:T(8,128)}, f32[256,128]{1,0:T(8,128)S(1)}, u32[]{:S(2)}, u32[]{:S(2)}) %collective-permute-start.6) | collective-permute-done | bytes 131104 | tf_op jit(solution)/shard_map/ppermute | solution.py:197
  236.2 10.3 %compress_node.5 = (f32[128,256]{1,0:T(8,128)}, f32[256,128]{1,0:T(8,128)}) custom-call(s32[2]{0:T(128)} %pad_add_fusion.2.rank_ref, f32[256,128]{1,0:T(8,128)} %get-tuple-element.16.mine_ref, f32[256,128]{1,0:T(8,128)} %copy-done.5, f32[256,128]{1,0:T(8,128)} %get-tuple-element.28.weights_ref), custom_call_target="tpu_custom_call" | custom-call | tf_op jit(solution)/shard_map/compress_node/pallas_call | solution.py:101
  246.5 1.9 collective-permute-start.7
  248.4 0.9 bitcast_dynamic-update-slice_fusion.2
  249.3 8.4 %collective-permute-done.7.other_ref = f32[256,128]{1,0:T(8,128)S(1)} collective-permute-done((f32[256,128]{1,0:T(8,128)}, f32[256,128]{1,0:T(8,128)S(1)}, u32[]{:S(2)}, u32[]{:S(2)}) %collective-permute-start.7) | collective-permute-done | bytes 131104 | tf_op jit(solution)/shard_map/ppermute | solution.py:197
  258.3 10.3 %compress_node.6 = (f32[128,256]{1,0:T(8,128)}, f32[256,128]{1,0:T(8,128)}) custom-call(s32[2]{0:T(128)} %pad_add_fusion.3.rank_ref, f32[256,128]{1,0:T(8,128)} %get-tuple-element.18.mine_ref, f32[256,128]{1,0:T(8,128)} %copy-done.4, f32[256,128]{1,0:T(8,128)} %get-tuple-element.31.weights_ref), custom_call_target="tpu_custom_call" | custom-call | tf_op jit(solution)/shard_map/compress_node/pallas_call | solution.py:101
  268.6 2.1 collective-permute-start.8
  270.8 0.9 bitcast_dynamic-update-slice_fusion.1
  271.7 13.7 %collective-permute-done.8 = f32[256,128]{1,0:T(8,128)S(1)} collective-permute-done((f32[256,128]{1,0:T(8,128)}, f32[256,128]{1,0:T(8,128)S(1)}, u32[]{:S(2)}, u32[]{:S(2)}) %collective-permute-start.8) | collective-permute-done | bytes 131104 | tf_op jit(solution)/shard_map/ppermute | solution.py:197
  285.3 9.5 %compress_node.7 = (f32[5,128,256]{2,1,0:T(8,128)S(1)}, f32[256,128]{1,0:T(8,128)S(1)}) fusion(f32[5,128,256]{2,1,0:T(8,128)S(1)} %bitcast_dynamic-update-slice_fusion.1, s32[2]{0:T(128)S(1)} %pad_add_fusion.4, f32[256,128]{1,0:T(8,128)} %get-tuple-element.20, f32[256,128]{1,0:T(8,128)S(1)} %collective-permute-done.8, f32[256,128]{1,0:T(8,128)S(1)} %get-tuple-element.27), kind=kCustom, calls=%fused_computation.25 | custom fusion | bytes 655872 | tf_op jit(solution)/shard_map/compress_node/pallas_call | solution.py:101
  294.9 4.1 %collective-permute-start.9 = (f32[16,128]{1,0:T(8,128)S(1)}, f32[16,128]{1,0:T(8,128)S(1)}, u32[]{:S(2)}, u32[]{:S(2)}) collective-permute-start(f32[16,128]{1,0:T(8,128)S(1)} %constant_dynamic-slice_fusion), channel_id=1, source_target_pairs={{0,256},{32,288},{64,320},{96,352},{128,384},{160,416},{192,448},{... | collective-permute-start | bytes 24584 | tf_op jit(solution)/shard_map/ppermute | solution.py:205
  299.0 9.0 %collective-permute-done.9 = f32[16,128]{1,0:T(8,128)S(1)} collective-permute-done((f32[16,128]{1,0:T(8,128)S(1)}, f32[16,128]{1,0:T(8,128)S(1)}, u32[]{:S(2)}, u32[]{:S(2)}) %collective-permute-start.9) | collective-permute-done | bytes 8224 | tf_op jit(solution)/shard_map/ppermute | solution.py:205
  (34 shorter events, 5.1 us)
Async XLA Ops:
  0.6 1.1 copy-start
  5.4 11.0 %collective-permute-start = (f32[128,2048]{1,0:T(8,128)S(1)}, f32[128,2048]{1,0:T(8,128)S(1)}, u32[]{:S(2)}, u32[]{:S(2)}) collective-permute-start(f32[128,2048]{1,0:T(8,128)S(1)} %convolution_multiply_fusion), channel_id=1, source_target_pairs={{0,1},{1,0},{2,3},{3,2},{4,5},{5,4},{6,7},{7,6},{8,9},{9,8},{10,11... | collective-permute-start | bytes 3145736 | tf_op jit(solution)/shard_map/ppermute | solution.py:114
  52.8 5.6 %collective-permute-start.1 = (bf16[128,2048]{1,0:T(8,128)(2,1)S(1)}, bf16[128,2048]{1,0:T(8,128)(2,1)S(1)}, u32[]{:S(2)}, u32[]{:S(2)}) collective-permute-start(bf16[128,2048]{1,0:T(8,128)(2,1)S(1)} %bitcast.48), channel_id=1, source_target_pairs={{0,1},{1,0},{2,3},{3,2},{4,5},{5,4},{6,7},{7,6},{8,9},{9,8},{10,11... | collective-permute-start | bytes 1572872 | tf_op jit(solution)/shard_map/ppermute | solution.py:114
  61.9 16.3 %collective-permute-start.2 = (f32[128,1024]{1,0:T(8,128)S(1)}, f32[128,1024]{1,0:T(8,128)S(1)}, u32[]{:S(2)}, u32[]{:S(2)}) collective-permute-start(f32[128,1024]{1,0:T(8,128)S(1)} %constant_dynamic-slice_fusion.1), channel_id=1, source_target_pairs={{0,32},{1,481},{32,0},{33,65},{64,96},{65,33},{96,64},{97,129},{12... | collective-permute-start | bytes 1572872 | tf_op jit(solution)/shard_map/ppermute | solution.py:169
  139.1 8.3 %collective-permute-start.3 = (bf16[128,1024]{1,0:T(8,128)(2,1)S(1)}, bf16[128,1024]{1,0:T(8,128)(2,1)S(1)}, u32[]{:S(2)}, u32[]{:S(2)}) collective-permute-start(bf16[128,1024]{1,0:T(8,128)(2,1)S(1)} %bitcast.50), channel_id=1, source_target_pairs={{0,32},{1,481},{32,0},{33,65},{64,96},{65,33},{96,64},{97,129},{12... | collective-permute-start | bytes 786440 | tf_op jit(solution)/shard_map/ppermute | solution.py:173
  149.8 6.6 %collective-permute-start.4 = (f32[256,1024]{1,0:T(8,128)S(1)}, f32[256,1024]{1,0:T(8,128)S(1)}, u32[]{:S(2)}, u32[]{:S(2)}) collective-permute-start(f32[256,1024]{1,0:T(8,128)S(1)} %fusion.12), channel_id=1, source_target_pairs={{0,1},{1,0},{2,3},{3,2},{4,5},{5,4},{6,7},{7,6},{8,9},{9,8},{10,11... | collective-permute-start | bytes 3145736 | tf_op jit(solution)/shard_map/ppermute | solution.py:114
  158.8 24.0 %copy-start.7 = (s32[6]{0:T(128)S(1)}, s32[6]{0:T(128)}, u32[]{:S(2)}) copy-start(s32[6]{0:T(128)} %param.9) | copy-start | bytes 76
  158.8 28.4 %copy-start.2 = (f32[6,256,128]{2,1,0:T(8,128)S(1)}, f32[6,256,128]{2,1,0:T(8,128)}, u32[]{:S(2)}) copy-start(f32[6,256,128]{2,1,0:T(8,128)} %param.8) | copy-start | bytes 2359300
  179.1 18.9 %all-to-all-start.5 = ((f32[16,16,1024]{2,1,0:T(8,128)}), f32[16,16,1024]{2,1,0:T(8,128)S(1)}, u32[]{:S(2)}, u32[]{:S(2)}) async-start(f32[16,16,1024]{2,1,0:T(8,128)} %broadcast_in_dim.30), calls=%async_computation.5 | async-start | bytes 2097152 | tf_op jit(solution)/shard_map/all_to_all | solution.py:118
  198.0 1.0 copy-start.1
  210.2 7.3 %collective-permute-start.5 = (f32[256,128]{1,0:T(8,128)}, f32[256,128]{1,0:T(8,128)S(1)}, u32[]{:S(2)}, u32[]{:S(2)}) collective-permute-start(f32[256,128]{1,0:T(8,128)} %get-tuple-element.14.mine_ref), channel_id=1, source_target_pairs={{0,1},{1,0},{2,3},{3,2},{4,5},{5,4},{6,7},{7,6},{8,9},{9,8},{10,11... | collective-permute-start | bytes 393224 | tf_op jit(solution)/shard_map/ppermute | solution.py:114
  217.4 0.7 copy-start.3
  228.4 7.1 %collective-permute-start.6 = (f32[256,128]{1,0:T(8,128)}, f32[256,128]{1,0:T(8,128)S(1)}, u32[]{:S(2)}, u32[]{:S(2)}) collective-permute-start(f32[256,128]{1,0:T(8,128)} %get-tuple-element.16.mine_ref), channel_id=1, source_target_pairs={{0,32},{32,0},{64,96},{96,64},{128,160},{160,128},{192,224},{224,1... | collective-permute-start | bytes 393224 | tf_op jit(solution)/shard_map/ppermute | solution.py:197
  235.5 0.7 copy-start.5
  246.5 11.2 %collective-permute-start.7 = (f32[256,128]{1,0:T(8,128)}, f32[256,128]{1,0:T(8,128)S(1)}, u32[]{:S(2)}, u32[]{:S(2)}) collective-permute-start(f32[256,128]{1,0:T(8,128)} %get-tuple-element.18.mine_ref), channel_id=1, source_target_pairs={{0,64},{32,96},{64,0},{96,32},{128,192},{160,224},{192,128},{224,1... | collective-permute-start | bytes 393224 | tf_op jit(solution)/shard_map/ppermute | solution.py:197
  257.7 0.7 copy-start.4
  268.6 16.7 %collective-permute-start.8 = (f32[256,128]{1,0:T(8,128)}, f32[256,128]{1,0:T(8,128)S(1)}, u32[]{:S(2)}, u32[]{:S(2)}) collective-permute-start(f32[256,128]{1,0:T(8,128)} %get-tuple-element.20), channel_id=1, source_target_pairs={{0,128},{32,160},{64,192},{96,224},{128,0},{160,32},{192,64},{224,... | collective-permute-start | bytes 393224 | tf_op jit(solution)/shard_map/ppermute | solution.py:197
  294.9 13.1 %collective-permute-start.9 = (f32[16,128]{1,0:T(8,128)S(1)}, f32[16,128]{1,0:T(8,128)S(1)}, u32[]{:S(2)}, u32[]{:S(2)}) collective-permute-start(f32[16,128]{1,0:T(8,128)S(1)} %constant_dynamic-slice_fusion), channel_id=1, source_target_pairs={{0,256},{32,288},{64,320},{96,352},{128,384},{160,416},{192,448},{... | collective-permute-start | bytes 24584 | tf_op jit(solution)/shard_map/ppermute | solution.py:205
  299.0 9.6 %copy-start.6 = (f32[5,128,256]{2,1,0:T(8,128)}, f32[5,128,256]{2,1,0:T(8,128)S(1)}, u32[]{:S(2)}) copy-start(f32[5,128,256]{2,1,0:T(8,128)S(1)} %broadcast_dynamic-update-slice_fusion) | copy-start | bytes 1966084

commit v2 on v1

--- a/solution.py
+++ b/solution.py
@@ -1,3 +1,5 @@
+import functools
+
 import jax
 import jax.numpy as jnp
 from jax import lax
@@ -8,7 +10,9 @@
 HIGHEST = lax.Precision.HIGHEST
 COLS = (((1,), (1,)), ((), ()))
 ROWS = (((0,), (0,)), ((), ()))
-ROW_BLOCK = 8
+ROW_BLOCK = 16
+LANES = 128
+VMEM_LIMIT = 16 << 20
 
 
 def exact_dot(a, b, dims):
@@ -51,13 +55,10 @@
         if b + 1 < count:
             scaled = panel * inverse
             outside = (lane < start) | (lane >= stop)
-            update = exact_dot(scaled[:, stop : stop + ROW_BLOCK], panel, ROWS)
-            panels[b + 1] = jnp.where(outside, panels[b + 1], 0.0) - update
-            if b + 2 < count:
-                update = exact_dot(scaled[:, stop + ROW_BLOCK :], panel, ROWS)
-                for i in range(b + 2, count):
-                    at = ROW_BLOCK * (i - b - 2)
-                    panels[i] = jnp.where(outside, panels[i], 0.0) - update[at : at + ROW_BLOCK, :]
+            update = exact_dot(scaled[:, stop:], panel, ROWS)
+            for i in range(b + 1, count):
+                at = ROW_BLOCK * (i - b - 1)
+                panels[i] = jnp.where(outside, panels[i], 0.0) - update[at : at + ROW_BLOCK, :]
     return jnp.concatenate(finished, axis=0)
 
 
@@ -75,51 +76,122 @@
     return bases, exact_dot(cross, inverse, COLS)
 
 
-def leaf_kernel(rank_ref, columns_ref, weights_ref, basis_ref, reduced_ref):
-    bases, reduced = compress_values([columns_ref[...]], weights_ref[...], rank_ref[0])
+def leaf_kernel(level, table_ref, columns_ref, weights_ref, basis_ref, reduced_ref):
+    rank = table_ref[level, 0]
+    columns = jnp.concatenate([decode(columns_ref[i]) for i in range(columns_ref.shape[0])], axis=0)
+    bases, reduced = compress_values([columns], weights_ref[...], rank)
     basis_ref[...] = bases[0]
     reduced_ref[...] = reduced
 
 
-def node_kernel(rank_ref, mine_ref, other_ref, weights_ref, basis_ref, reduced_ref):
-    upper = rank_ref[1] == 1
+def node_kernel(level, table_ref, mine_ref, other_ref, weights_ref, basis_ref, reduced_ref):
+    upper = table_ref[level, 1] == 1
     mine = mine_ref[...]
     other = other_ref[...]
     parts = [jnp.where(upper, other, mine), jnp.where(upper, mine, other)]
-    bases, reduced = compress_values(parts, weights_ref[...], rank_ref[0])
+    bases, reduced = compress_values(parts, weights_ref[...], table_ref[level, 0])
     top = weights_ref.shape[1]
     basis_ref[:, :top] = bases[0]
     basis_ref[:, top:] = bases[1]
     reduced_ref[...] = reduced
 
 
-def compress(scalars, parts, weights):
+def compress(level, table, parts, weights):
     samples, top = weights.shape
-    width = sum(part.shape[1] for part in parts)
+    width = parts[0].shape[-1] - LANES if len(parts) == 1 else 2 * top
     kernel = leaf_kernel if len(parts) == 1 else node_kernel
     vmem = pl.BlockSpec(memory_space=pltpu.VMEM)
     return pl.pallas_call(
-        kernel,
+        functools.partial(kernel, level),
         in_specs=[pl.BlockSpec(memory_space=pltpu.SMEM)] + [vmem] * (len(parts) + 1),
         out_specs=(vmem, vmem),
         out_shape=(
             jax.ShapeDtypeStruct((top, width), jnp.float32),
             jax.ShapeDtypeStruct((samples, top), jnp.float32),
         ),
+        compiler_params=pltpu.CompilerParams(vmem_limit_bytes=VMEM_LIMIT),
         name="compress_leaf" if len(parts) == 1 else "compress_node",
-    )(scalars, *parts, weights)
+    )(table, *parts, weights)
 
 
 def swap_cores(x):
     return lax.ppermute(x, "cblk", [(0, 1), (1, 0)])
 
 
-def exchange(x, axis, groups=None):
-    return lax.all_to_all(x, axis, 0, 0, axis_index_groups=groups)
-
-
-def spread(x, count, axis, groups=None):
-    return exchange(jnp.broadcast_to(x[None], (count,) + x.shape), axis, groups)
+def exchange(x, axis):
+    return lax.all_to_all(x, axis, 0, 0)
+
+
+def encode(x):
+    lane = lax.broadcasted_iota(jnp.int32, (x.shape[0], LANES), 1)
+    tail = jnp.zeros((x.shape[0], LANES), jnp.float32)
+    tiles = []
+    for g in range(x.shape[1] // LANES):
+        tile = x[:, g * LANES : (g + 1) * LANES]
+        top = jnp.max(jnp.abs(tile), axis=1, keepdims=True)
+        bits = jnp.clip(14.0 - jnp.ceil(jnp.log2(top)), -120.0, 120.0)
+        bits = jnp.broadcast_to(jnp.where(top > 0, bits, 0.0), tile.shape)
+        tiles.append(jnp.round(tile * jnp.exp2(bits)))
+        tail = jnp.where(lane == g, bits, tail)
+    return jnp.concatenate(tiles + [tail], axis=1).astype(jnp.int32).astype(jnp.int16)
+
+
+def decode(message):
+    wide = message.astype(jnp.int32).astype(jnp.float32)
+    width = wide.shape[1] - LANES
+    scale = jnp.exp2(-wide[:, width:])
+    return jnp.concatenate(
+        [
+            wide[:, g * LANES : (g + 1) * LANES] * scale[:, g : g + 1]
+            for g in range(width // LANES)
+        ],
+        axis=1,
+    )
+
+
+def encode_kernel(*refs):
+    out_ref = refs[-1]
+    count, rows, _ = out_ref.shape
+    for i in range(count):
+        at = pl.ds(i * rows, rows)
+        out_ref[i] = encode(sum(ref[at, :] for ref in refs[:-1]))
+
+
+def merge_kernel(message_ref, out_ref):
+    total = decode(message_ref[0])
+    for i in range(1, message_ref.shape[0]):
+        total = total + decode(message_ref[i])
+    if out_ref.dtype == jnp.int16:
+        value = encode(total)
+    else:
+        value = total.astype(out_ref.dtype)
+    for i in range(out_ref.shape[0]):
+        out_ref[i] = value
+
+
+def packed(parts, count):
+    rows, width = parts[0].shape
+    out = jax.ShapeDtypeStruct((count, rows // count, width + LANES), jnp.int16)
+    return whole_call(encode_kernel, parts, out, "encode")
+
+
+def merged(message, dtype):
+    count, rows, width = message.shape
+    width = width if dtype == jnp.int16 else width - LANES
+    out = jax.ShapeDtypeStruct((count, rows, width), dtype)
+    return whole_call(merge_kernel, [message], out, "merge")
+
+
+def whole_call(kernel, operands, out, name):
+    vmem = pl.BlockSpec(memory_space=pltpu.VMEM)
+    return pl.pallas_call(
+        kernel,
+        in_specs=[vmem] * len(operands),
+        out_specs=vmem,
+        out_shape=out,
+        compiler_params=pltpu.CompilerParams(vmem_limit_bytes=VMEM_LIMIT),
+        name=name,
+    )(*operands)
 
 
 def body(front, pattern, sample, sketch, level_ranks):
@@ -146,10 +218,9 @@
         return lax.dot_general(part, front, COLS, preferred_element_type=f32)
 
     away = swap_cores(first_half(1 - c) * leaf_mask.astype(f32))
-    total = first_half(c) * leaf_mask.astype(f32) + away
-    pieces = exchange(total.reshape(n_samp, half // n_samp, rows), "samp")
-    piece = jnp.sum(pieces, axis=0).astype(bf16)
-    mine = spread(piece, n_samp, "samp").reshape(half, rows)
+    message = packed([first_half(c) * leaf_mask.astype(f32), away], n_samp)
+    pieces = merged(exchange(message, "samp"), bf16)
+    mine = exchange(pieces, "samp").reshape(half, rows)
     other = swap_cores(mine)
     first_sample = jnp.where(
         c == 0, jnp.concatenate([mine, other], 0), jnp.concatenate([other, mine], 0)
@@ -157,23 +228,8 @@
     first_sample = first_sample * leaf_mask.astype(bf16)
 
     back_part = jnp.dot(first_sample, front, preferred_element_type=f32)
-    odd = z % 2
-    pairs = []
-    for i in range(n_leaf):
-        pairs.append((2 * i, 2 * (i ^ 1)))
-        pairs.append((2 * i + 1, 2 * ((i + 1 if i % 2 else i - 1) % n_leaf) + 1))
-    group = n_leaf // 2
-    parity = [list(range(p, n_leaf, 2)) for p in range(2)]
-    given = lax.dynamic_slice_in_dim(back_part, (1 - odd) * half, half, 0)
-    kept = lax.dynamic_slice_in_dim(back_part, odd * half, half, 0)
-    kept = kept + lax.ppermute(given, ("leaf", "cblk"), pairs)
-    pieces = exchange(kept.reshape(group, half // group, width), "leaf", parity)
-    piece = jnp.sum(pieces, axis=0).astype(bf16)
-    mine = spread(piece, group, "leaf", parity).reshape(half, width)
-    other = lax.ppermute(mine, ("leaf", "cblk"), pairs)
-    back_sample = jnp.where(
-        odd == 0, jnp.concatenate([mine, other], 0), jnp.concatenate([other, mine], 0)
-    )
+    pieces = merged(exchange(packed([back_part], n_leaf), "leaf"), bf16)
+    back_sample = exchange(pieces, "leaf").reshape(samples, width)
 
     def third_half(which):
         part = lax.dynamic_slice_in_dim(front, which * leaf_rows, leaf_rows, 0)
@@ -181,23 +237,18 @@
         return lax.dot_general(back_sample, part, COLS, preferred_element_type=f32) * flag
 
     away = swap_cores(third_half(1 - c))
-    total = third_half(c) + away
-    pieces = exchange(total.reshape(n_samp, samples // n_samp, leaf_rows), "samp")
-    piece = jnp.sum(pieces, axis=0)
-    leaf_columns = spread(piece, n_samp, "samp").reshape(samples, leaf_rows)
-
-    def scalars(level, upper):
-        return jnp.stack([level_ranks[level], upper.astype(jnp.int32)])
-
-    leaf_basis, reduced = compress(scalars(0, c), [leaf_columns], sketch[0])
+    message = packed([third_half(c), away], n_samp)
+    columns = exchange(merged(exchange(message, "samp"), jnp.int16), "samp")
+
+    uppers = [c, c] + [z // 2**bit % 2 for bit in range(depth - 1)]
+    table = jnp.stack([level_ranks[: len(uppers)], jnp.stack(uppers).astype(jnp.int32)], axis=1)
+    leaf_basis, reduced = compress(0, table, [columns], sketch[0])
     path = []
-    node_basis, reduced = compress(scalars(1, c), [reduced, swap_cores(reduced)], sketch[1])
+    node_basis, reduced = compress(1, table, [reduced, swap_cores(reduced)], sketch[1])
     path.append(node_basis)
     for bit in range(depth - 1):
         partner = lax.ppermute(reduced, "leaf", [(i, i ^ (1 << bit)) for i in range(n_leaf)])
-        node_basis, reduced = compress(
-            scalars(bit + 2, z // 2**bit % 2), [reduced, partner], sketch[bit + 2]
-        )
+        node_basis, reduced = compress(bit + 2, table, [reduced, partner], sketch[bit + 2])
         path.append(node_basis)
     share = samples // n_samp
     mine = lax.dynamic_slice_in_dim(reduced, s * share, share, 0)

time: 310 us -> 269 us (0.87)
  blocking collectives: 113 us -> 74.5 us
  waiting for transfers between devices: 60.6 us -> 73.8 us
  local copies, waits for them, and re-layouts: 19.5 us -> 9.68 us
  Pallas kernels: 42.1 us -> 34 us
  starting transfers between devices: 47.7 us -> 55.8 us
  other arithmetic: 8.42 us -> 2.44 us
    all_to_all x5 -> x3, blocking collectives: 113 us -> 74.5 us  [exchange(): return lax.all_to_all(x, axis, 0, 0)]
    all_to_all x1 -> x3, waiting for transfers between devices: 9.97 us -> 42.1 us  [exchange(): return lax.all_to_all(x, axis, 0, 0)]
    ppermute x2 -> x0, starting transfers between devices: 11.6 us -> none  [the longest x1 9.72 us: body(): kept = kept + lax.ppermute(given, ('leaf', 'cblk'), pairs)]
    ppermute x2 -> x0, waiting for transfers between devices: 10.9 us -> none  [the longest x1 6.55 us: body(): kept = kept + lax.ppermute(given, ('leaf', 'cblk'), pairs)]
    pallas_call x4 -> x10, Pallas kernels: 42.1 us -> 34 us  [the longest x4 28.3 us: compress(): pl.pallas_call(functools.partial(kernel, level), in_specs=[pl.BlockSpec(m...]
    all_to_all x1 -> x3, starting transfers between devices: 3.65 us -> 11.7 us  [exchange(): return lax.all_to_all(x, axis, 0, 0)]
    another operation x5 -> x1, other arithmetic: 5.78 us -> 0.01 us  [body(): jnp.stack([level_ranks[:len(uppers)], jnp.stack(uppers).astype(jnp.int32)...]
    unnamed x23 -> x13, local copies, waits for them, and re-layouts: 5.89 us -> 0.24 us
  transfers between devices with their start and end apart: 11 -> 11, of which waited for: 10 -> 9; matrix products, arithmetic and copies ran while one was open for 4% -> 4% of each run, Pallas kernels for 0% -> 0%
where the time goes in v2:
time: 269 us; the launch traced here: 268 us
  blocking collectives  74.5 us (28%)
  waiting for transfers between devices  73.8 us (27%)
  starting transfers between devices  55.8 us (21%)
  Pallas kernels  34 us (13%)
  matrix products  15.5 us (6%)
  local copies, waits for them, and re-layouts  9.68 us (4%)
    all_to_all x3, blocking collectives, exchange(): return lax.all_to_all(x, axis, 0, 0)  74.5 us
    all_to_all x3, waiting for transfers between devices, exchange(): return lax.all_to_all(x, axis, 0, 0)  42.1 us
    pallas_call x4, Pallas kernels, compress(): pl.pallas_call(functools.partial(kernel, level), in_specs=[pl.BlockSpec(m...  28.3 us
    ppermute x4, starting transfers between devices, swap_cores(): return lax.ppermute(x, 'cblk', [(0, 1), (1, 0)])  25.7 us
    ppermute x3, waiting for transfers between devices, body(): lax.ppermute(reduced, 'leaf', [(i, i ^ 1 << bit) for i in range(n_leaf)])  24.1 us
    all_to_all x3, starting transfers between devices, exchange(): return lax.all_to_all(x, axis, 0, 0)  11.7 us
    ppermute x3, starting transfers between devices, body(): lax.ppermute(reduced, 'leaf', [(i, i ^ 1 << bit) for i in range(n_leaf)])  11.5 us
    dot_general x2, matrix products, first_half(): return lax.dot_general(part, front, COLS, preferred_element_type=f32)  7.4 us
  transfers between devices with their start and end apart: 11, of which 9 were waited for; matrix products, arithmetic and copies ran while one was open for 4% of the time, Pallas kernels for 0%

profile of v2, /device:TPU:1, one launch (start us, length us, event | category | flops | bytes accessed | tf_op | source)
XLA Modules:
  0.0 268.2 jit_solution(12903200162222159927)
XLA Ops:
  0.7 0.9 convert_reduce_fusion
  1.6 0.1 broadcast_bitcast_fusion
  1.7 3.7 %convolution_multiply_fusion = f32[128,2048]{1,0:T(8,128)S(1)} fusion(bf16[2048,1024]{1,0:T(8,128)(2,1)} %param.5, f32[2048]{0:T(1024)S(1)} %bitcast.49, bf16[256,1024]{1,0:T(8,128)(2,1)S(1)} %copy-done, s32[]{:T(128)S(6)} %select_n.94), kind=kOutput, calls=%fused_computation | convolution fusion | flops 537133056 | bytes 5513220 | tf_op jit(solution)/shard_map/dot_general | solution.py:218
  5.4 8.7 %collective-permute-start = (f32[128,2048]{1,0:T(8,128)S(1)}, f32[128,2048]{1,0:T(8,128)S(1)}, u32[]{:S(2)}, u32[]{:S(2)}) collective-permute-start(f32[128,2048]{1,0:T(8,128)S(1)} %convolution_multiply_fusion), channel_id=1, source_target_pairs={{0,1},{1,0},{2,3},{3,2},{4,5},{5,4},{6,7},{7,6},{8,9},{9,8},{10,11... | collective-permute-start | bytes 3145736 | tf_op jit(solution)/shard_map/ppermute | solution.py:118
  14.2 3.7 %convolution_multiply_fusion.1.refs_0_ = f32[128,2048]{1,0:T(8,128)S(1)} fusion(bf16[2048,1024]{1,0:T(8,128)(2,1)} %param.5, f32[2048]{0:T(1024)S(1)} %bitcast.50, bf16[256,1024]{1,0:T(8,128)(2,1)S(1)} %copy-done, s32[]{:T(128)S(6)} %select_n.91), kind=kOutput, calls=%fused_computation.1 | convolution fusion | flops 537133056 | bytes 5513220 | tf_op jit(solution)/shard_map/dot_general | solution.py:218
  17.9 0.5 encode.3
  18.4 14.6 %all_to_all.30.message_ref = s16[16,8,2176]{2,1,0:T(8,128)(2,1)S(1)} all-to-all(s16[16,8,2176]{2,1,0:T(8,128)(2,1)S(1)} %encode.3), channel_id=1, replica_groups=mesh['leaf'=16,'samp'=16,'cblk'=2] {'samp'}, dimensions={0} | all-to-all | bytes 1114112 | tf_op jit(solution)/shard_map/all_to_all | solution.py:122
  33.0 0.5 merge.3
  33.6 13.2 %all_to_all.31 = bf16[16,8,2048]{2,1,0:T(8,128)(2,1)S(1)} all-to-all(bf16[16,8,2048]{2,1,0:T(8,128)(2,1)S(1)} %merge.3), channel_id=1, replica_groups=mesh['leaf'=16,'samp'=16,'cblk'=2] {'samp'}, dimensions={0} | all-to-all | bytes 1048576 | tf_op jit(solution)/shard_map/all_to_all | solution.py:122
  46.7 4.0 %collective-permute-start.1 = (bf16[128,2048]{1,0:T(8,128)(2,1)S(1)}, bf16[128,2048]{1,0:T(8,128)(2,1)S(1)}, u32[]{:S(2)}, u32[]{:S(2)}) collective-permute-start(bf16[128,2048]{1,0:T(8,128)(2,1)S(1)} %bitcast.47), channel_id=1, source_target_pairs={{0,1},{1,0},{2,3},{3,2},{4,5},{5,4},{6,7},{7,6},{8,9},{9,8},{10,11... | collective-permute-start | bytes 1572872 | tf_op jit(solution)/shard_map/ppermute | solution.py:118
  50.7 0.9 convert_reduce_fusion.1
  51.6 0.1 broadcast_bitcast_fusion.1
  51.7 0.5 collective-permute-done.1
  52.3 3.5 %fusion.11.refs_0_ = f32[256,1024]{1,0:T(8,128)S(1)} fusion(bf16[2048,1024]{1,0:T(8,128)(2,1)} %param.5, bf16[128,2048]{1,0:T(8,128)(2,1)S(1)} %collective-permute-done.1, bf16[128,2048]{1,0:T(8,128)(2,1)S(1)} %bitcast.48, pred[]{:T(512)S(6)} %eq.11, bf16[2048]{0:T(1024)(128)(2,1)S(1)} %bitcast.52), kind=kOutput, calls=%fused_computation.10 | convolution fusion | flops 1080557568 | bytes 6295553 | tf_op jit(solution)/shard_map/dot_general | solution.py:230
  55.7 0.5 encode.4
  56.2 46.8 %all_to_all.32.message_ref = s16[16,16,1152]{2,1,0:T(8,128)(2,1)S(1)} all-to-all(s16[16,16,1152]{2,1,0:T(8,128)(2,1)S(1)} %encode.4), channel_id=1, replica_groups=mesh['leaf'=16,'samp'=16,'cblk'=2] {'leaf'}, dimensions={0} | all-to-all | bytes 1179648 | tf_op jit(solution)/shard_map/all_to_all | solution.py:122
  103.0 1.3 merge.4
  104.3 4.4 %all-to-all-start.3 = ((bf16[16,16,1024]{2,1,0:T(8,128)(2,1)}), bf16[16,16,1024]{2,1,0:T(8,128)(2,1)S(1)}, u32[]{:S(2)}, u32[]{:S(2)}) async-start(bf16[16,16,1024]{2,1,0:T(8,128)(2,1)} %merge.4), calls=%async_computation.3 | async-start | bytes 1048576 | tf_op jit(solution)/shard_map/all_to_all | solution.py:122
  108.7 1.4 fusion.30
  110.8 20.9 %all-to-all-done.3 = bf16[16,16,1024]{2,1,0:T(8,128)(2,1)S(1)} async-done(((bf16[16,16,1024]{2,1,0:T(8,128)(2,1)}), bf16[16,16,1024]{2,1,0:T(8,128)(2,1)S(1)}, u32[]{:S(2)}, u32[]{:S(2)}) %all-to-all-start.3) | async-done | bytes 524320 | tf_op jit(solution)/shard_map/all_to_all | solution.py:122
  131.7 2.3 fusion.7
  134.0 8.8 %collective-permute-start.2 = (f32[256,1024]{1,0:T(8,128)S(1)}, f32[256,1024]{1,0:T(8,128)S(1)}, u32[]{:S(2)}, u32[]{:S(2)}) collective-permute-start(f32[256,1024]{1,0:T(8,128)S(1)} %fusion.7), channel_id=1, source_target_pairs={{0,1},{1,0},{2,3},{3,2},{4,5},{5,4},{6,7},{7,6},{8,9},{9,8},{10,11... | collective-permute-start | bytes 3145736 | tf_op jit(solution)/shard_map/ppermute | solution.py:118
  143.5 2.3 fusion.4.refs_0_
  145.9 1.3 encode.5
  147.2 3.6 %all-to-all-start.4 = ((s16[16,16,1152]{2,1,0:T(8,128)(2,1)}), s16[16,16,1152]{2,1,0:T(8,128)(2,1)S(1)}, u32[]{:S(2)}, u32[]{:S(2)}) async-start(s16[16,16,1152]{2,1,0:T(8,128)(2,1)} %encode.5), calls=%async_computation.4 | async-start | bytes 1179648 | tf_op jit(solution)/shard_map/all_to_all | solution.py:122
  150.9 0.1 stack.45
  151.0 11.8 %all-to-all-done.4.message_ref = s16[16,16,1152]{2,1,0:T(8,128)(2,1)S(1)} async-done(((s16[16,16,1152]{2,1,0:T(8,128)(2,1)}), s16[16,16,1152]{2,1,0:T(8,128)(2,1)S(1)}, u32[]{:S(2)}, u32[]{:S(2)}) %all-to-all-start.4) | async-done | bytes 589856 | tf_op jit(solution)/shard_map/all_to_all | solution.py:122
  162.8 1.4 merge.5
  164.3 3.8 %all-to-all-start.5 = ((s16[16,16,1152]{2,1,0:T(8,128)(2,1)}), s16[16,16,1152]{2,1,0:T(8,128)(2,1)S(1)}, u32[]{:S(2)}, u32[]{:S(2)}) async-start(s16[16,16,1152]{2,1,0:T(8,128)(2,1)} %merge.5), calls=%async_computation.5 | async-start | bytes 1179648 | tf_op jit(solution)/shard_map/all_to_all | solution.py:122
  168.1 0.1 copy.10.table_ref
  168.2 1.2 slice_bitcast_fusion
  169.4 9.4 %all-to-all-done.5.columns_ref = s16[16,16,1152]{2,1,0:T(8,128)(2,1)S(1)} async-done(((s16[16,16,1152]{2,1,0:T(8,128)(2,1)}), s16[16,16,1152]{2,1,0:T(8,128)(2,1)S(1)}, u32[]{:S(2)}, u32[]{:S(2)}) %all-to-all-start.5) | async-done | bytes 589856 | tf_op jit(solution)/shard_map/all_to_all | solution.py:122
  178.7 8.5 %compress_leaf.1 = (f32[128,1024]{1,0:T(8,128)}, f32[256,128]{1,0:T(8,128)S(1)}) custom-call(s32[5,2]{1,0:T(8,128)S(1)} %copy.10.table_ref, s16[16,16,1152]{2,1,0:T(8,128)(2,1)S(1)} %all-to-all-done.5.columns_ref, f32[256,128]{1,0:T(8,128)S(1)} %get-tuple-element.30.weights_ref), custom_call_target="tpu_custom_call" | custom-call | tf_op jit(solution)/shard_map/compress_leaf/pallas_call | solution.py:104
  187.3 4.2 %collective-permute-start.3 = (f32[256,128]{1,0:T(8,128)S(1)}, f32[256,128]{1,0:T(8,128)S(1)}, u32[]{:S(2)}, u32[]{:S(2)}) collective-permute-start(f32[256,128]{1,0:T(8,128)S(1)} %get-tuple-element.14.mine_ref), channel_id=1, source_target_pairs={{0,1},{1,0},{2,3},{3,2},{4,5},{5,4},{6,7},{7,6},{8,9},{9,8},{10,11... | collective-permute-start | bytes 393224 | tf_op jit(solution)/shard_map/ppermute | solution.py:118
  191.5 0.9 collective-permute-done.3.other_ref
  192.4 6.6 %compress_node.4 = (f32[128,256]{1,0:T(8,128)S(1)}, f32[256,128]{1,0:T(8,128)S(1)}) custom-call(s32[5,2]{1,0:T(8,128)S(1)} %copy.10.table_ref, f32[256,128]{1,0:T(8,128)S(1)} %get-tuple-element.14.mine_ref, f32[256,128]{1,0:T(8,128)S(1)} %collective-permute-done.3.other_ref, f32[256,128]{1,0:T(8,128)S(1)} %get-tuple-element.29.weights_ref), custom_call_target="tpu_custom_call" | custom-call | tf_op jit(solution)/shard_map/compress_node/pallas_call | solution.py:104
  199.0 2.8 %collective-permute-start.4 = (f32[256,128]{1,0:T(8,128)S(1)}, f32[256,128]{1,0:T(8,128)S(1)}, u32[]{:S(2)}, u32[]{:S(2)}) collective-permute-start(f32[256,128]{1,0:T(8,128)S(1)} %get-tuple-element.16.mine_ref), channel_id=1, source_target_pairs={{0,32},{32,0},{64,96},{96,64},{128,160},{160,128},{192,224},{224,1... | collective-permute-start | bytes 393224 | tf_op jit(solution)/shard_map/ppermute | solution.py:250
  201.8 3.8 %collective-permute-done.4.other_ref = f32[256,128]{1,0:T(8,128)S(1)} collective-permute-done((f32[256,128]{1,0:T(8,128)S(1)}, f32[256,128]{1,0:T(8,128)S(1)}, u32[]{:S(2)}, u32[]{:S(2)}) %collective-permute-start.4) | collective-permute-done | bytes 131104 | tf_op jit(solution)/shard_map/ppermute | solution.py:250
  205.6 6.6 %compress_node.5 = (f32[128,256]{1,0:T(8,128)S(1)}, f32[256,128]{1,0:T(8,128)S(1)}) custom-call(s32[5,2]{1,0:T(8,128)S(1)} %copy.10.table_ref, f32[256,128]{1,0:T(8,128)S(1)} %get-tuple-element.16.mine_ref, f32[256,128]{1,0:T(8,128)S(1)} %collective-permute-done.4.other_ref, f32[256,128]{1,0:T(8,128)S(1)} %get-tuple-element.28.weights_ref), custom_call_target="tpu_custom_call" | custom-call | tf_op jit(solution)/shard_map/compress_node/pallas_call | solution.py:104
  212.2 4.0 %collective-permute-start.5 = (f32[256,128]{1,0:T(8,128)S(1)}, f32[256,128]{1,0:T(8,128)S(1)}, u32[]{:S(2)}, u32[]{:S(2)}) collective-permute-start(f32[256,128]{1,0:T(8,128)S(1)} %get-tuple-element.18.mine_ref), channel_id=1, source_target_pairs={{0,64},{32,96},{64,0},{96,32},{128,192},{160,224},{192,128},{224,1... | collective-permute-start | bytes 393224 | tf_op jit(solution)/shard_map/ppermute | solution.py:250
  216.3 6.4 %collective-permute-done.5.other_ref = f32[256,128]{1,0:T(8,128)S(1)} collective-permute-done((f32[256,128]{1,0:T(8,128)S(1)}, f32[256,128]{1,0:T(8,128)S(1)}, u32[]{:S(2)}, u32[]{:S(2)}) %collective-permute-start.5) | collective-permute-done | bytes 131104 | tf_op jit(solution)/shard_map/ppermute | solution.py:250
  222.6 6.6 %compress_node.6 = (f32[128,256]{1,0:T(8,128)S(1)}, f32[256,128]{1,0:T(8,128)S(1)}) custom-call(s32[5,2]{1,0:T(8,128)S(1)} %copy.10.table_ref, f32[256,128]{1,0:T(8,128)S(1)} %get-tuple-element.18.mine_ref, f32[256,128]{1,0:T(8,128)S(1)} %collective-permute-done.5.other_ref, f32[256,128]{1,0:T(8,128)S(1)} %get-tuple-element.31.weights_ref), custom_call_target="tpu_custom_call" | custom-call | tf_op jit(solution)/shard_map/compress_node/pallas_call | solution.py:104
  229.2 4.7 %collective-permute-start.6 = (f32[256,128]{1,0:T(8,128)S(1)}, f32[256,128]{1,0:T(8,128)S(1)}, u32[]{:S(2)}, u32[]{:S(2)}) collective-permute-start(f32[256,128]{1,0:T(8,128)S(1)} %get-tuple-element.20), channel_id=1, source_target_pairs={{0,128},{32,160},{64,192},{96,224},{128,0},{160,32},{192,64},{224,... | collective-permute-start | bytes 393224 | tf_op jit(solution)/shard_map/ppermute | solution.py:250
  234.0 13.9 %collective-permute-done.6 = f32[256,128]{1,0:T(8,128)S(1)} collective-permute-done((f32[256,128]{1,0:T(8,128)S(1)}, f32[256,128]{1,0:T(8,128)S(1)}, u32[]{:S(2)}, u32[]{:S(2)}) %collective-permute-start.6) | collective-permute-done | bytes 131104 | tf_op jit(solution)/shard_map/ppermute | solution.py:250
  247.9 6.6 %compress_node.7 = (f32[5,128,256]{2,1,0:T(8,128)S(1)}, f32[256,128]{1,0:T(8,128)S(1)}) fusion(f32[5,128,256]{2,1,0:T(8,128)S(1)} %bitcast_dynamic-update-slice_fusion.1, s32[5,2]{1,0:T(8,128)S(1)} %copy.10.table_ref, f32[256,128]{1,0:T(8,128)S(1)} %get-tuple-element.20, f32[256,128]{1,0:T(8,128)S(1)} %collective-permute-done.6, ...), kind=kCustom, calls=%fused_computation.20 | custom fusion | bytes 659456 | tf_op jit(solution)/shard_map/compress_node/pallas_call | solution.py:104
  254.5 6.9 %collective-permute-start.7 = (f32[16,128]{1,0:T(8,128)S(1)}, f32[16,128]{1,0:T(8,128)S(1)}, u32[]{:S(2)}, u32[]{:S(2)}) collective-permute-start(f32[16,128]{1,0:T(8,128)S(1)} %constant_dynamic-slice_fusion), channel_id=1, source_target_pairs={{0,256},{32,288},{64,320},{96,352},{128,384},{160,416},{192,448},{... | collective-permute-start | bytes 24584 | tf_op jit(solution)/shard_map/ppermute | solution.py:256
  261.5 6.1 %collective-permute-done.7 = f32[16,128]{1,0:T(8,128)S(1)} collective-permute-done((f32[16,128]{1,0:T(8,128)S(1)}, f32[16,128]{1,0:T(8,128)S(1)}, u32[]{:S(2)}, u32[]{:S(2)}) %collective-permute-start.7) | collective-permute-done | bytes 8224 | tf_op jit(solution)/shard_map/ppermute | solution.py:256
  267.6 0.6 pad_maximum_fusion
  (18 shorter events, 0.1 us)
Async XLA Ops:
  0.6 1.1 copy-start
  5.4 12.5 %collective-permute-start = (f32[128,2048]{1,0:T(8,128)S(1)}, f32[128,2048]{1,0:T(8,128)S(1)}, u32[]{:S(2)}, u32[]{:S(2)}) collective-permute-start(f32[128,2048]{1,0:T(8,128)S(1)} %convolution_multiply_fusion), channel_id=1, source_target_pairs={{0,1},{1,0},{2,3},{3,2},{4,5},{5,4},{6,7},{7,6},{8,9},{9,8},{10,11... | collective-permute-start | bytes 3145736 | tf_op jit(solution)/shard_map/ppermute | solution.py:118
  46.7 5.5 %collective-permute-start.1 = (bf16[128,2048]{1,0:T(8,128)(2,1)S(1)}, bf16[128,2048]{1,0:T(8,128)(2,1)S(1)}, u32[]{:S(2)}, u32[]{:S(2)}) collective-permute-start(bf16[128,2048]{1,0:T(8,128)(2,1)S(1)} %bitcast.47), channel_id=1, source_target_pairs={{0,1},{1,0},{2,3},{3,2},{4,5},{5,4},{6,7},{7,6},{8,9},{9,8},{10,11... | collective-permute-start | bytes 1572872 | tf_op jit(solution)/shard_map/ppermute | solution.py:118
  104.3 27.4 %all-to-all-start.3 = ((bf16[16,16,1024]{2,1,0:T(8,128)(2,1)}), bf16[16,16,1024]{2,1,0:T(8,128)(2,1)S(1)}, u32[]{:S(2)}, u32[]{:S(2)}) async-start(bf16[16,16,1024]{2,1,0:T(8,128)(2,1)} %merge.4), calls=%async_computation.3 | async-start | bytes 1048576 | tf_op jit(solution)/shard_map/all_to_all | solution.py:122
  134.0 11.9 %collective-permute-start.2 = (f32[256,1024]{1,0:T(8,128)S(1)}, f32[256,1024]{1,0:T(8,128)S(1)}, u32[]{:S(2)}, u32[]{:S(2)}) collective-permute-start(f32[256,1024]{1,0:T(8,128)S(1)} %fusion.7), channel_id=1, source_target_pairs={{0,1},{1,0},{2,3},{3,2},{4,5},{5,4},{6,7},{7,6},{8,9},{9,8},{10,11... | collective-permute-start | bytes 3145736 | tf_op jit(solution)/shard_map/ppermute | solution.py:118
  143.5 24.5 %copy-start.2 = (s32[6]{0:T(128)S(1)}, s32[6]{0:T(128)}, u32[]{:S(2)}) copy-start(s32[6]{0:T(128)} %param.9) | copy-start | bytes 76
  147.2 15.6 %all-to-all-start.4 = ((s16[16,16,1152]{2,1,0:T(8,128)(2,1)}), s16[16,16,1152]{2,1,0:T(8,128)(2,1)S(1)}, u32[]{:S(2)}, u32[]{:S(2)}) async-start(s16[16,16,1152]{2,1,0:T(8,128)(2,1)} %encode.5), calls=%async_computation.4 | async-start | bytes 1179648 | tf_op jit(solution)/shard_map/all_to_all | solution.py:122
  164.3 14.5 %all-to-all-start.5 = ((s16[16,16,1152]{2,1,0:T(8,128)(2,1)}), s16[16,16,1152]{2,1,0:T(8,128)(2,1)S(1)}, u32[]{:S(2)}, u32[]{:S(2)}) async-start(s16[16,16,1152]{2,1,0:T(8,128)(2,1)} %merge.5), calls=%async_computation.5 | async-start | bytes 1179648 | tf_op jit(solution)/shard_map/all_to_all | solution.py:122
  187.3 5.1 %collective-permute-start.3 = (f32[256,128]{1,0:T(8,128)S(1)}, f32[256,128]{1,0:T(8,128)S(1)}, u32[]{:S(2)}, u32[]{:S(2)}) collective-permute-start(f32[256,128]{1,0:T(8,128)S(1)} %get-tuple-element.14.mine_ref), channel_id=1, source_target_pairs={{0,1},{1,0},{2,3},{3,2},{4,5},{5,4},{6,7},{7,6},{8,9},{9,8},{10,11... | collective-permute-start | bytes 393224 | tf_op jit(solution)/shard_map/ppermute | solution.py:118
  199.0 6.6 %collective-permute-start.4 = (f32[256,128]{1,0:T(8,128)S(1)}, f32[256,128]{1,0:T(8,128)S(1)}, u32[]{:S(2)}, u32[]{:S(2)}) collective-permute-start(f32[256,128]{1,0:T(8,128)S(1)} %get-tuple-element.16.mine_ref), channel_id=1, source_target_pairs={{0,32},{32,0},{64,96},{96,64},{128,160},{160,128},{192,224},{224,1... | collective-permute-start | bytes 393224 | tf_op jit(solution)/shard_map/ppermute | solution.py:250
  212.2 10.5 %collective-permute-start.5 = (f32[256,128]{1,0:T(8,128)S(1)}, f32[256,128]{1,0:T(8,128)S(1)}, u32[]{:S(2)}, u32[]{:S(2)}) collective-permute-start(f32[256,128]{1,0:T(8,128)S(1)} %get-tuple-element.18.mine_ref), channel_id=1, source_target_pairs={{0,64},{32,96},{64,0},{96,32},{128,192},{160,224},{192,128},{224,1... | collective-permute-start | bytes 393224 | tf_op jit(solution)/shard_map/ppermute | solution.py:250
  229.2 18.6 %collective-permute-start.6 = (f32[256,128]{1,0:T(8,128)S(1)}, f32[256,128]{1,0:T(8,128)S(1)}, u32[]{:S(2)}, u32[]{:S(2)}) collective-permute-start(f32[256,128]{1,0:T(8,128)S(1)} %get-tuple-element.20), channel_id=1, source_target_pairs={{0,128},{32,160},{64,192},{96,224},{128,0},{160,32},{192,64},{224,... | collective-permute-start | bytes 393224 | tf_op jit(solution)/shard_map/ppermute | solution.py:250
  254.5 13.1 %collective-permute-start.7 = (f32[16,128]{1,0:T(8,128)S(1)}, f32[16,128]{1,0:T(8,128)S(1)}, u32[]{:S(2)}, u32[]{:S(2)}) collective-permute-start(f32[16,128]{1,0:T(8,128)S(1)} %constant_dynamic-slice_fusion), channel_id=1, source_target_pairs={{0,256},{32,288},{64,320},{96,352},{128,384},{160,416},{192,448},{... | collective-permute-start | bytes 24584 | tf_op jit(solution)/shard_map/ppermute | solution.py:256
  261.4 6.8 %copy-start.1 = (f32[5,128,256]{2,1,0:T(8,128)}, f32[5,128,256]{2,1,0:T(8,128)S(1)}, u32[]{:S(2)}) copy-start(f32[5,128,256]{2,1,0:T(8,128)S(1)} %broadcast_dynamic-update-slice_fusion) | copy-start | bytes 1966084

commit v3 on v2

--- a/solution.py
+++ b/solution.py
@@ -12,6 +12,8 @@
 ROWS = (((0,), (0,)), ((), ()))
 ROW_BLOCK = 16
 LANES = 128
+FOLD = 8
+TILE = 8
 VMEM_LIMIT = 16 << 20
 
 
@@ -76,39 +78,60 @@
     return bases, exact_dot(cross, inverse, COLS)
 
 
-def leaf_kernel(level, table_ref, columns_ref, weights_ref, basis_ref, reduced_ref):
+def fold(x):
+    rows = x.shape[0] // FOLD
+    return jnp.concatenate([x[i * rows : (i + 1) * rows, :] for i in range(FOLD)], axis=1)
+
+
+def unfold(x):
+    width = x.shape[1] // FOLD
+    return jnp.concatenate([x[:, i * width : (i + 1) * width] for i in range(FOLD)], axis=0)
+
+
+def leaf_kernel(level, table_ref, columns_ref, weights_ref, basis_ref, reduced_ref, message_ref):
     rank = table_ref[level, 0]
-    columns = jnp.concatenate([decode(columns_ref[i]) for i in range(columns_ref.shape[0])], axis=0)
+    share = weights_ref.shape[0] // columns_ref.shape[0]
+    columns = jnp.concatenate(
+        [stacked_rows(decode(columns_ref[i]), share) for i in range(columns_ref.shape[0])], axis=0
+    )
     bases, reduced = compress_values([columns], weights_ref[...], rank)
     basis_ref[...] = bases[0]
     reduced_ref[...] = reduced
-
-
-def node_kernel(level, table_ref, mine_ref, other_ref, weights_ref, basis_ref, reduced_ref):
+    message_ref[...] = encode(fold(reduced))
+
+
+def node_kernel(
+    level, table_ref, mine_ref, other_ref, weights_ref, basis_ref, reduced_ref, message_ref=None
+):
     upper = table_ref[level, 1] == 1
     mine = mine_ref[...]
-    other = other_ref[...]
+    other = unfold(decode(other_ref[...]))
     parts = [jnp.where(upper, other, mine), jnp.where(upper, mine, other)]
     bases, reduced = compress_values(parts, weights_ref[...], table_ref[level, 0])
     top = weights_ref.shape[1]
     basis_ref[:, :top] = bases[0]
     basis_ref[:, top:] = bases[1]
     reduced_ref[...] = reduced
-
-
-def compress(level, table, parts, weights):
+    if message_ref is not None:
+        message_ref[...] = encode(fold(reduced))
+
+
+def compress(level, table, parts, weights, last=False):
     samples, top = weights.shape
-    width = parts[0].shape[-1] - LANES if len(parts) == 1 else 2 * top
+    width = (parts[0].shape[-1] - LANES) * parts[0].shape[0] * TILE // samples if len(parts) == 1 else 2 * top
     kernel = leaf_kernel if len(parts) == 1 else node_kernel
     vmem = pl.BlockSpec(memory_space=pltpu.VMEM)
+    outs = [
+        jax.ShapeDtypeStruct((top, width), jnp.float32),
+        jax.ShapeDtypeStruct((samples, top), jnp.float32),
+        jax.ShapeDtypeStruct((samples // FOLD, FOLD * top + LANES), jnp.int16),
+    ]
+    outs = outs[:2] if last else outs
     return pl.pallas_call(
         functools.partial(kernel, level),
         in_specs=[pl.BlockSpec(memory_space=pltpu.SMEM)] + [vmem] * (len(parts) + 1),
-        out_specs=(vmem, vmem),
-        out_shape=(
-            jax.ShapeDtypeStruct((top, width), jnp.float32),
-            jax.ShapeDtypeStruct((samples, top), jnp.float32),
-        ),
+        out_specs=(vmem,) * len(outs),
+        out_shape=tuple(outs),
         compiler_params=pltpu.CompilerParams(vmem_limit_bytes=VMEM_LIMIT),
         name="compress_leaf" if len(parts) == 1 else "compress_node",
     )(table, *parts, weights)
@@ -118,8 +141,8 @@
     return lax.ppermute(x, "cblk", [(0, 1), (1, 0)])
 
 
-def exchange(x, axis):
-    return lax.all_to_all(x, axis, 0, 0)
+def exchange(x, axis, groups=None):
+    return lax.all_to_all(x, axis, 0, 0, axis_index_groups=groups)
 
 
 def encode(x):
@@ -129,7 +152,7 @@
     for g in range(x.shape[1] // LANES):
         tile = x[:, g * LANES : (g + 1) * LANES]
         top = jnp.max(jnp.abs(tile), axis=1, keepdims=True)
-        bits = jnp.clip(14.0 - jnp.ceil(jnp.log2(top)), -120.0, 120.0)
+        bits = jnp.clip(15.0 - jnp.ceil(jnp.log2(top * 1.001)), -120.0, 120.0)
         bits = jnp.broadcast_to(jnp.where(top > 0, bits, 0.0), tile.shape)
         tiles.append(jnp.round(tile * jnp.exp2(bits)))
         tail = jnp.where(lane == g, bits, tail)
@@ -149,12 +172,42 @@
     )
 
 
+def side_by_side(x):
+    return jnp.concatenate([x[:TILE, :], x[TILE:, :]], axis=1) if x.shape[0] > TILE else x
+
+
+def stacked_rows(x, rows):
+    if rows == TILE:
+        return x
+    width = x.shape[1] // 2
+    return jnp.concatenate([x[:, :width], x[:, width:]], axis=0)
+
+
 def encode_kernel(*refs):
     out_ref = refs[-1]
-    count, rows, _ = out_ref.shape
+    count = out_ref.shape[0]
+    rows = refs[0].shape[0] // count
     for i in range(count):
         at = pl.ds(i * rows, rows)
-        out_ref[i] = encode(sum(ref[at, :] for ref in refs[:-1]))
+        out_ref[i] = encode(side_by_side(sum(ref[at, :] for ref in refs[:-1])))
+
+
+def give_kernel(parity_ref, part_ref, out_ref):
+    count = out_ref.shape[0]
+    rows = part_ref.shape[0] // (2 * count)
+    other = 1 - parity_ref[0]
+    for i in range(count):
+        at = pl.multiple_of((2 * i + other) * rows, rows)
+        out_ref[i] = encode(side_by_side(part_ref[pl.ds(at, rows), :]))
+
+
+def keep_kernel(parity_ref, part_ref, message_ref, out_ref):
+    count = out_ref.shape[0]
+    rows = part_ref.shape[0] // (2 * count)
+    for i in range(count):
+        at = pl.multiple_of((2 * i + parity_ref[0]) * rows, rows)
+        kept = side_by_side(part_ref[pl.ds(at, rows), :])
+        out_ref[i] = encode(kept + decode(message_ref[i]))
 
 
 def merge_kernel(message_ref, out_ref):
@@ -164,34 +217,41 @@
     if out_ref.dtype == jnp.int16:
         value = encode(total)
     else:
-        value = total.astype(out_ref.dtype)
+        value = stacked_rows(total, out_ref.shape[1]).astype(out_ref.dtype)
     for i in range(out_ref.shape[0]):
         out_ref[i] = value
 
 
+def message_of(count, values):
+    return jax.ShapeDtypeStruct((count, TILE, values // TILE + LANES), jnp.int16)
+
+
 def packed(parts, count):
-    rows, width = parts[0].shape
-    out = jax.ShapeDtypeStruct((count, rows // count, width + LANES), jnp.int16)
+    out = message_of(count, parts[0].size // count)
     return whole_call(encode_kernel, parts, out, "encode")
 
 
-def merged(message, dtype):
-    count, rows, width = message.shape
-    width = width if dtype == jnp.int16 else width - LANES
-    out = jax.ShapeDtypeStruct((count, rows, width), dtype)
+def merged(message, count, rows, width):
+    out = jax.ShapeDtypeStruct((count, rows, width), jnp.bfloat16)
     return whole_call(merge_kernel, [message], out, "merge")
 
 
-def whole_call(kernel, operands, out, name):
+def merged_again(message, count):
+    out = jax.ShapeDtypeStruct((count,) + message.shape[1:], jnp.int16)
+    return whole_call(merge_kernel, [message], out, "merge")
+
+
+def whole_call(kernel, operands, out, name, scalars=()):
     vmem = pl.BlockSpec(memory_space=pltpu.VMEM)
+    smem = pl.BlockSpec(memory_space=pltpu.SMEM)
     return pl.pallas_call(
         kernel,
-        in_specs=[vmem] * len(operands),
+        in_specs=[smem] * len(scalars) + [vmem] * len(operands),
         out_specs=vmem,
         out_shape=out,
         compiler_params=pltpu.CompilerParams(vmem_limit_bytes=VMEM_LIMIT),
         name=name,
-    )(*operands)
+    )(*scalars, *operands)
 
 
 def body(front, pattern, sample, sketch, level_ranks):
@@ -215,11 +275,12 @@
 
     def first_half(which):
         part = lax.dynamic_slice_in_dim(sample, which * half, half, 0)
-        return lax.dot_general(part, front, COLS, preferred_element_type=f32)
-
-    away = swap_cores(first_half(1 - c) * leaf_mask.astype(f32))
-    message = packed([first_half(c) * leaf_mask.astype(f32), away], n_samp)
-    pieces = merged(exchange(message, "samp"), bf16)
+        part = lax.dot_general(part, front, COLS, preferred_element_type=f32)
+        return part * leaf_mask.astype(f32)
+
+    away = swap_cores(first_half(1 - c))
+    message = packed([first_half(c), away], n_samp)
+    pieces = merged(exchange(message, "samp"), n_samp, half // n_samp, rows)
     mine = exchange(pieces, "samp").reshape(half, rows)
     other = swap_cores(mine)
     first_sample = jnp.where(
@@ -228,7 +289,18 @@
     first_sample = first_sample * leaf_mask.astype(bf16)
 
     back_part = jnp.dot(first_sample, front, preferred_element_type=f32)
-    pieces = merged(exchange(packed([back_part], n_leaf), "leaf"), bf16)
+    parity = (z % 2).astype(jnp.int32).reshape(1)
+    pairs = []
+    for i in range(n_leaf):
+        pairs.append((2 * i, 2 * (i ^ 1)))
+        pairs.append((2 * i + 1, 2 * ((i + 1 if i % 2 else i - 1) % n_leaf) + 1))
+    group = n_leaf // 2
+    form = message_of(group, samples // n_leaf * width)
+    given = whole_call(give_kernel, [back_part], form, "give", [parity])
+    given = lax.ppermute(given, ("leaf", "cblk"), pairs)
+    message = whole_call(keep_kernel, [back_part, given], form, "keep", [parity])
+    same = [list(range(p, n_leaf, 2)) for p in range(2)]
+    pieces = merged(exchange(message, "leaf", same), n_leaf, samples // n_leaf, width)
     back_sample = exchange(pieces, "leaf").reshape(samples, width)
 
     def third_half(which):
@@ -238,18 +310,22 @@
 
     away = swap_cores(third_half(1 - c))
     message = packed([third_half(c), away], n_samp)
-    columns = exchange(merged(exchange(message, "samp"), jnp.int16), "samp")
+    columns = exchange(merged_again(exchange(message, "samp"), n_samp), "samp")
 
     uppers = [c, c] + [z // 2**bit % 2 for bit in range(depth - 1)]
     table = jnp.stack([level_ranks[: len(uppers)], jnp.stack(uppers).astype(jnp.int32)], axis=1)
-    leaf_basis, reduced = compress(0, table, [columns], sketch[0])
+    leaf_basis, reduced, message = compress(0, table, [columns], sketch[0])
     path = []
-    node_basis, reduced = compress(1, table, [reduced, swap_cores(reduced)], sketch[1])
-    path.append(node_basis)
-    for bit in range(depth - 1):
-        partner = lax.ppermute(reduced, "leaf", [(i, i ^ (1 << bit)) for i in range(n_leaf)])
-        node_basis, reduced = compress(bit + 2, table, [reduced, partner], sketch[bit + 2])
+    partner = swap_cores(message)
+    for level in range(1, depth + 1):
+        last = level == depth
+        node_basis, reduced, *message = compress(
+            level, table, [reduced, partner], sketch[level], last
+        )
         path.append(node_basis)
+        if not last:
+            pairs = [(i, i ^ (1 << (level - 1))) for i in range(n_leaf)]
+            partner = lax.ppermute(message[0], "leaf", pairs)
     share = samples // n_samp
     mine = lax.dynamic_slice_in_dim(reduced, s * share, share, 0)
     bit = depth - 1

time: 269 us -> 255 us (0.948); the launches traced: 268 us -> 250 us
  blocking collectives: 74.5 us -> 57 us
  local copies, waits for them, and re-layouts: 9.68 us -> 23.2 us
  Pallas kernels: 34 us -> 21.5 us
  waiting for transfers between devices: 73.8 us -> 64.8 us
  starting transfers between devices: 55.8 us -> 63.6 us
    all_to_all x3, blocking collectives: 74.5 us -> 57 us  [exchange(): return lax.all_to_all(x, axis, 0, 0, axis_index_groups=groups)]
    pallas_call x1 -> x3, local copies, waits for them, and re-layouts: 6.59 us -> 20.2 us  [compress(): pl.pallas_call(functools.partial(kernel, level), in_specs=[pl.BlockSpec(m...]
    pallas_call x4 -> x2, Pallas kernels: 28.3 us -> 15.3 us  [compress(): pl.pallas_call(functools.partial(kernel, level), in_specs=[pl.BlockSpec(m...]
    ppermute x3 -> x4, starting transfers between devices: 11.5 us -> 20.9 us  [the longest x3 11.4 us: body(): partner = lax.ppermute(message[0], 'leaf', pairs)]
    ppermute x3 -> x4, waiting for transfers between devices: 24.1 us -> 14.9 us  [the longest x3 11 us: body(): partner = lax.ppermute(message[0], 'leaf', pairs)]
    pallas_call x6 -> x7, Pallas kernels: 5.66 us -> 6.2 us  [whole_call(): pl.pallas_call(kernel, in_specs=[smem] * len(scalars) + [vmem] * len(oper...]
  transfers between devices with their start and end apart: 11 -> 12, of which waited for: 9 -> 10; matrix products, arithmetic and copies ran while one was open for 4% -> 4% of each run, Pallas kernels for 0% -> 0%
where the time goes in v3:
time: 255 us; the launch traced here: 250 us
  waiting for transfers between devices  64.8 us (25%)
  starting transfers between devices  63.6 us (25%)
  blocking collectives  57 us (22%)
  local copies, waits for them, and re-layouts  23.2 us (9%)
  Pallas kernels  21.5 us (8%)
  matrix products  15.5 us (6%)
    all_to_all x3, blocking collectives, exchange(): return lax.all_to_all(x, axis, 0, 0, axis_index_groups=groups)  57 us
    all_to_all x3, waiting for transfers between devices, exchange(): return lax.all_to_all(x, axis, 0, 0, axis_index_groups=groups)  41.8 us
    ppermute x4, starting transfers between devices, swap_cores(): return lax.ppermute(x, 'cblk', [(0, 1), (1, 0)])  25.3 us
    pallas_call x3, local copies, waits for them, and re-layouts, compress(): pl.pallas_call(functools.partial(kernel, level), in_specs=[pl.BlockSpec(m...  20.2 us
    pallas_call x2, Pallas kernels, compress(): pl.pallas_call(functools.partial(kernel, level), in_specs=[pl.BlockSpec(m...  15.3 us
    ppermute x3, starting transfers between devices, body(): partner = lax.ppermute(message[0], 'leaf', pairs)  11.4 us
    ppermute x3, waiting for transfers between devices, body(): partner = lax.ppermute(message[0], 'leaf', pairs)  11 us
    all_to_all x3, starting transfers between devices, exchange(): return lax.all_to_all(x, axis, 0, 0, axis_index_groups=groups)  10.9 us
  transfers between devices with their start and end apart: 12, of which 10 were waited for; matrix products, arithmetic and copies ran while one was open for 4% of the time, Pallas kernels for 0%

profile of v3, /device:TPU:1, one launch (start us, length us, event | category | flops | bytes accessed | tf_op | source)
XLA Modules:
  0.0 250.4 jit_solution(18131589617490327532)
XLA Ops:
  0.7 0.9 convert_reduce_fusion
  1.7 3.7 %convolution_multiply_fusion = f32[128,2048]{1,0:T(8,128)S(1)} fusion(bf16[2048,1024]{1,0:T(8,128)(2,1)} %param.5, f32[2048]{0:T(1024)S(1)} %bitcast.49, bf16[256,1024]{1,0:T(8,128)(2,1)S(1)} %copy-done, s32[]{:T(128)S(6)} %select_n.96), kind=kOutput, calls=%fused_computation | convolution fusion | flops 537133056 | bytes 5513220 | tf_op jit(solution)/shard_map/dot_general | solution.py:278
  5.4 8.7 %collective-permute-start = (f32[128,2048]{1,0:T(8,128)S(1)}, f32[128,2048]{1,0:T(8,128)S(1)}, u32[]{:S(2)}, u32[]{:S(2)}) collective-permute-start(f32[128,2048]{1,0:T(8,128)S(1)} %convolution_multiply_fusion), channel_id=1, source_target_pairs={{0,1},{1,0},{2,3},{3,2},{4,5},{5,4},{6,7},{7,6},{8,9},{9,8},{10,11... | collective-permute-start | bytes 3145736 | tf_op jit(solution)/shard_map/ppermute | solution.py:141
  14.2 3.7 %convolution_multiply_fusion.1.refs_0_ = f32[128,2048]{1,0:T(8,128)S(1)} fusion(bf16[2048,1024]{1,0:T(8,128)(2,1)} %param.5, f32[2048]{0:T(1024)S(1)} %bitcast.50, bf16[256,1024]{1,0:T(8,128)(2,1)S(1)} %copy-done, s32[]{:T(128)S(6)} %select_n.93), kind=kOutput, calls=%fused_computation.1 | convolution fusion | flops 537133056 | bytes 5513220 | tf_op jit(solution)/shard_map/dot_general | solution.py:278
  17.9 0.6 encode.2
  18.4 14.6 %all_to_all.30.message_ref = s16[16,8,2176]{2,1,0:T(8,128)(2,1)S(1)} all-to-all(s16[16,8,2176]{2,1,0:T(8,128)(2,1)S(1)} %encode.2), channel_id=1, replica_groups=mesh['leaf'=16,'samp'=16,'cblk'=2] {'samp'}, dimensions={0} | all-to-all | bytes 1114112 | tf_op jit(solution)/shard_map/all_to_all | solution.py:145
  33.0 0.5 merge.3
  33.6 13.2 %all_to_all.31 = bf16[16,8,2048]{2,1,0:T(8,128)(2,1)S(1)} all-to-all(bf16[16,8,2048]{2,1,0:T(8,128)(2,1)S(1)} %merge.3), channel_id=1, replica_groups=mesh['leaf'=16,'samp'=16,'cblk'=2] {'samp'}, dimensions={0} | all-to-all | bytes 1048576 | tf_op jit(solution)/shard_map/all_to_all | solution.py:145
  46.8 4.0 %collective-permute-start.1 = (bf16[128,2048]{1,0:T(8,128)(2,1)S(1)}, bf16[128,2048]{1,0:T(8,128)(2,1)S(1)}, u32[]{:S(2)}, u32[]{:S(2)}) collective-permute-start(bf16[128,2048]{1,0:T(8,128)(2,1)S(1)} %bitcast.47), channel_id=1, source_target_pairs={{0,1},{1,0},{2,3},{3,2},{4,5},{5,4},{6,7},{7,6},{8,9},{9,8},{10,11... | collective-permute-start | bytes 1572872 | tf_op jit(solution)/shard_map/ppermute | solution.py:141
  50.8 0.9 convert_reduce_fusion.1
  51.7 0.5 collective-permute-done.1
  52.3 3.5 %fusion.11.part_ref = f32[256,1024]{1,0:T(8,128)S(1)} fusion(bf16[2048,1024]{1,0:T(8,128)(2,1)} %param.5, bf16[128,2048]{1,0:T(8,128)(2,1)S(1)} %collective-permute-done.1, bf16[128,2048]{1,0:T(8,128)(2,1)S(1)} %bitcast.48, pred[]{:T(512)S(6)} %eq.12, bf16[2048]{0:T(1024)(128)(2,1)S(1)} %bitcast.52), kind=kOutput, calls=%fused_computation.10 | convolution fusion | flops 1080557568 | bytes 6295553 | tf_op jit(solution)/shard_map/dot_general | solution.py:291
  55.8 0.3 give.1
  56.1 9.5 %collective-permute-start.2 = (s16[8,8,2176]{2,1,0:T(8,128)(2,1)S(1)}, s16[8,8,2176]{2,1,0:T(8,128)(2,1)S(1)}, u32[]{:S(2)}, u32[]{:S(2)}) collective-permute-start(s16[8,8,2176]{2,1,0:T(8,128)(2,1)S(1)} %give.1), channel_id=1, source_target_pairs={{0,32},{1,481},{32,0},{33,65},{64,96},{65,33},{96,64},{97,129},{12... | collective-permute-start | bytes 835592 | tf_op jit(solution)/shard_map/ppermute | solution.py:300
  65.6 3.9 %collective-permute-done.2.message_ref = s16[8,8,2176]{2,1,0:T(8,128)(2,1)S(1)} collective-permute-done((s16[8,8,2176]{2,1,0:T(8,128)(2,1)S(1)}, s16[8,8,2176]{2,1,0:T(8,128)(2,1)S(1)}, u32[]{:S(2)}, u32[]{:S(2)}) %collective-permute-start.2) | collective-permute-done | bytes 278560 | tf_op jit(solution)/shard_map/ppermute | solution.py:300
  69.5 0.9 keep.1
  70.4 29.2 %all_to_all.32.message_ref = s16[8,8,2176]{2,1,0:T(8,128)(2,1)S(1)} all-to-all(s16[8,8,2176]{2,1,0:T(8,128)(2,1)S(1)} %keep.1), channel_id=1, replica_groups={{0,64,128,192,256,320,384,448},{32,96,160,224,288,352,416,480},{1,65,12..., dimensions={0} | all-to-all | bytes 557056 | tf_op jit(solution)/shard_map/all_to_all | solution.py:145
  99.6 1.1 merge.4
  100.8 3.6 %all-to-all-start.3 = ((bf16[16,16,1024]{2,1,0:T(8,128)(2,1)}), bf16[16,16,1024]{2,1,0:T(8,128)(2,1)S(1)}, u32[]{:S(2)}, u32[]{:S(2)}) async-start(bf16[16,16,1024]{2,1,0:T(8,128)(2,1)} %merge.4), calls=%async_computation.3 | async-start | bytes 1048576 | tf_op jit(solution)/shard_map/all_to_all | solution.py:145
  104.4 1.4 fusion.38
  106.4 21.0 %all-to-all-done.3 = bf16[16,16,1024]{2,1,0:T(8,128)(2,1)S(1)} async-done(((bf16[16,16,1024]{2,1,0:T(8,128)(2,1)}), bf16[16,16,1024]{2,1,0:T(8,128)(2,1)S(1)}, u32[]{:S(2)}, u32[]{:S(2)}) %all-to-all-start.3) | async-done | bytes 524320 | tf_op jit(solution)/shard_map/all_to_all | solution.py:145
  127.4 2.3 fusion.7
  129.8 8.7 %collective-permute-start.3 = (f32[256,1024]{1,0:T(8,128)S(1)}, f32[256,1024]{1,0:T(8,128)S(1)}, u32[]{:S(2)}, u32[]{:S(2)}) collective-permute-start(f32[256,1024]{1,0:T(8,128)S(1)} %fusion.7), channel_id=1, source_target_pairs={{0,1},{1,0},{2,3},{3,2},{4,5},{5,4},{6,7},{7,6},{8,9},{9,8},{10,11... | collective-permute-start | bytes 3145736 | tf_op jit(solution)/shard_map/ppermute | solution.py:141
  139.1 2.3 fusion.4.refs_0_
  141.4 1.4 encode.3
  142.8 3.6 %all-to-all-start.4 = ((s16[16,8,2176]{2,1,0:T(8,128)(2,1)}), s16[16,8,2176]{2,1,0:T(8,128)(2,1)S(1)}, u32[]{:S(2)}, u32[]{:S(2)}) async-start(s16[16,8,2176]{2,1,0:T(8,128)(2,1)} %encode.3), calls=%async_computation.4 | async-start | bytes 1114112 | tf_op jit(solution)/shard_map/all_to_all | solution.py:145
  146.5 11.5 %all-to-all-done.4.message_ref = s16[16,8,2176]{2,1,0:T(8,128)(2,1)S(1)} async-done(((s16[16,8,2176]{2,1,0:T(8,128)(2,1)}), s16[16,8,2176]{2,1,0:T(8,128)(2,1)S(1)}, u32[]{:S(2)}, u32[]{:S(2)}) %all-to-all-start.4) | async-done | bytes 557088 | tf_op jit(solution)/shard_map/all_to_all | solution.py:145
  158.0 1.4 merge.5
  159.4 3.8 %all-to-all-start.5 = ((s16[16,8,2176]{2,1,0:T(8,128)(2,1)}), s16[16,8,2176]{2,1,0:T(8,128)(2,1)S(1)}, u32[]{:S(2)}, u32[]{:S(2)}) async-start(s16[16,8,2176]{2,1,0:T(8,128)(2,1)} %merge.5), calls=%async_computation.5 | async-start | bytes 1114112 | tf_op jit(solution)/shard_map/all_to_all | solution.py:145
  163.2 0.1 copy.10.table_ref
  163.3 1.2 slice_bitcast_fusion
  164.6 9.3 %all-to-all-done.5.columns_ref = s16[16,8,2176]{2,1,0:T(8,128)(2,1)S(1)} async-done(((s16[16,8,2176]{2,1,0:T(8,128)(2,1)}), s16[16,8,2176]{2,1,0:T(8,128)(2,1)S(1)}, u32[]{:S(2)}, u32[]{:S(2)}) %all-to-all-start.5) | async-done | bytes 557088 | tf_op jit(solution)/shard_map/all_to_all | solution.py:145
  173.9 8.6 %compress_leaf.1 = (f32[128,1024]{1,0:T(8,128)}, f32[256,128]{1,0:T(8,128)S(1)}, s16[32,1152]{1,0:T(8,128)(2,1)S(1)}) custom-call(s32[5,2]{1,0:T(8,128)S(1)} %copy.10.table_ref, s16[16,8,2176]{2,1,0:T(8,128)(2,1)S(1)} %all-to-all-done.5.columns_ref, f32[256,128]{1,0:T(8,128)S(1)} %get-tuple-element.50.weights_ref), custom_call_target="tpu_custom_call" | custom-call | tf_op jit(solution)/shard_map/compress_leaf/pallas_call | solution.py:130
  182.4 3.9 %collective-permute-start.4 = (s16[32,1152]{1,0:T(8,128)(2,1)S(1)}, s16[32,1152]{1,0:T(8,128)(2,1)S(1)}, u32[]{:S(2)}, u32[]{:S(2)}) collective-permute-start(s16[32,1152]{1,0:T(8,128)(2,1)S(1)} %get-tuple-element.19), channel_id=1, source_target_pairs={{0,1},{1,0},{2,3},{3,2},{4,5},{5,4},{6,7},{7,6},{8,9},{9,8},{10,11... | collective-permute-start | bytes 221192 | tf_op jit(solution)/shard_map/ppermute | solution.py:141
  186.3 0.9 collective-permute-done.4.other_ref
  187.2 6.8 %compress_node.4 = (f32[128,256]{1,0:T(8,128)S(1)}, f32[256,128]{1,0:T(8,128)S(1)}, s16[32,1152]{1,0:T(8,128)(2,1)S(1)}) custom-call(s32[5,2]{1,0:T(8,128)S(1)} %copy.10.table_ref, f32[256,128]{1,0:T(8,128)S(1)} %get-tuple-element.18.mine_ref, s16[32,1152]{1,0:T(8,128)(2,1)S(1)} %collective-permute-done.4.other_ref, f32[256,128]{1,0:T(8,128)S(1)} %get-tuple-element.49.weights_ref), custom_call_target="tpu_custom_call" | custom-call | tf_op jit(solution)/shard_map/compress_node/pallas_call | solution.py:130
  194.0 2.8 %collective-permute-start.5 = (s16[32,1152]{1,0:T(8,128)(2,1)S(1)}, s16[32,1152]{1,0:T(8,128)(2,1)S(1)}, u32[]{:S(2)}, u32[]{:S(2)}) collective-permute-start(s16[32,1152]{1,0:T(8,128)(2,1)S(1)} %get-tuple-element.22), channel_id=1, source_target_pairs={{0,32},{32,0},{64,96},{96,64},{128,160},{160,128},{192,224},{224,1... | collective-permute-start | bytes 221192 | tf_op jit(solution)/shard_map/ppermute | solution.py:328
  196.8 2.3 collective-permute-done.5
  199.1 6.8 %compress_node.7 = (f32[5,128,256]{2,1,0:T(8,128)S(1)}, f32[256,128]{1,0:T(8,128)S(1)}, s16[32,1152]{1,0:T(8,128)(2,1)S(1)}) fusion(f32[5,128,256]{2,1,0:T(8,128)S(1)} %bitcast_dynamic-update-slice_fusion.3, s32[5,2]{1,0:T(8,128)S(1)} %copy.10.table_ref, f32[256,128]{1,0:T(8,128)S(1)} %get-tuple-element.21, s16[32,1152]{1,0:T(8,128)(2,1)S(1)} %collective-permute-done.5, ...), kind=kCustom, calls=%fused_computation.22 | custom fusion | bytes 675840 | tf_op jit(solution)/shard_map/compress_node/pallas_call | solution.py:130
  205.8 4.3 %collective-permute-start.6 = (s16[32,1152]{1,0:T(8,128)(2,1)S(1)}, s16[32,1152]{1,0:T(8,128)(2,1)S(1)}, u32[]{:S(2)}, u32[]{:S(2)}) collective-permute-start(s16[32,1152]{1,0:T(8,128)(2,1)S(1)} %get-tuple-element.42), channel_id=1, source_target_pairs={{0,64},{32,96},{64,0},{96,32},{128,192},{160,224},{192,128},{224,1... | collective-permute-start | bytes 221192 | tf_op jit(solution)/shard_map/ppermute | solution.py:328
  210.2 2.5 collective-permute-done.6
  212.6 6.8 %compress_node.6 = (f32[5,128,256]{2,1,0:T(8,128)S(1)}, f32[256,128]{1,0:T(8,128)S(1)}, s16[32,1152]{1,0:T(8,128)(2,1)S(1)}) fusion(f32[5,128,256]{2,1,0:T(8,128)S(1)} %get-tuple-element.39, s32[5,2]{1,0:T(8,128)S(1)} %copy.10.table_ref, f32[256,128]{1,0:T(8,128)S(1)} %get-tuple-element.40, s16[32,1152]{1,0:T(8,128)(2,1)S(1)} %collective-permute-done.6, ...), kind=kCustom, calls=%fused_computation.21 | custom fusion | bytes 675840 | tf_op jit(solution)/shard_map/compress_node/pallas_call | solution.py:130
  219.4 4.3 %collective-permute-start.7 = (s16[32,1152]{1,0:T(8,128)(2,1)S(1)}, s16[32,1152]{1,0:T(8,128)(2,1)S(1)}, u32[]{:S(2)}, u32[]{:S(2)}) collective-permute-start(s16[32,1152]{1,0:T(8,128)(2,1)S(1)} %get-tuple-element.36), channel_id=1, source_target_pairs={{0,128},{32,160},{64,192},{96,224},{128,0},{160,32},{192,64},{224,... | collective-permute-start | bytes 221192 | tf_op jit(solution)/shard_map/ppermute | solution.py:328
  223.7 6.2 %collective-permute-done.7 = s16[32,1152]{1,0:T(8,128)(2,1)S(1)} collective-permute-done((s16[32,1152]{1,0:T(8,128)(2,1)S(1)}, s16[32,1152]{1,0:T(8,128)(2,1)S(1)}, u32[]{:S(2)}, u32[]{:S(2)}) %collective-permute-start.7) | collective-permute-done | bytes 73760 | tf_op jit(solution)/shard_map/ppermute | solution.py:328
  230.0 6.7 %compress_node.5 = (f32[5,128,256]{2,1,0:T(8,128)S(1)}, f32[256,128]{1,0:T(8,128)S(1)}) fusion(f32[5,128,256]{2,1,0:T(8,128)S(1)} %get-tuple-element.33, s32[5,2]{1,0:T(8,128)S(1)} %copy.10.table_ref, f32[256,128]{1,0:T(8,128)S(1)} %get-tuple-element.34, s16[32,1152]{1,0:T(8,128)(2,1)S(1)} %collective-permute-done.7, f32[256,128]{1,0:T(8,128)S(1)} %get-tuple-element.47), kind=kCustom, calls=%fused_computation.20 | custom fusion | bytes 602112 | tf_op jit(solution)/shard_map/compress_node/pallas_call | solution.py:130
  236.7 6.4 %collective-permute-start.8 = (f32[16,128]{1,0:T(8,128)S(1)}, f32[16,128]{1,0:T(8,128)S(1)}, u32[]{:S(2)}, u32[]{:S(2)}) collective-permute-start(f32[16,128]{1,0:T(8,128)S(1)} %constant_dynamic-slice_fusion), channel_id=1, source_target_pairs={{0,256},{32,288},{64,320},{96,352},{128,384},{160,416},{192,448},{... | collective-permute-start | bytes 24584 | tf_op jit(solution)/shard_map/ppermute | solution.py:332
  243.1 6.6 %collective-permute-done.8 = f32[16,128]{1,0:T(8,128)S(1)} collective-permute-done((f32[16,128]{1,0:T(8,128)S(1)}, f32[16,128]{1,0:T(8,128)S(1)}, u32[]{:S(2)}, u32[]{:S(2)}) %collective-permute-start.8) | collective-permute-done | bytes 8224 | tf_op jit(solution)/shard_map/ppermute | solution.py:332
  249.8 0.6 pad_maximum_fusion
  (19 shorter events, 0.3 us)
Async XLA Ops:
  0.6 1.1 copy-start
  5.4 12.5 %collective-permute-start = (f32[128,2048]{1,0:T(8,128)S(1)}, f32[128,2048]{1,0:T(8,128)S(1)}, u32[]{:S(2)}, u32[]{:S(2)}) collective-permute-start(f32[128,2048]{1,0:T(8,128)S(1)} %convolution_multiply_fusion), channel_id=1, source_target_pairs={{0,1},{1,0},{2,3},{3,2},{4,5},{5,4},{6,7},{7,6},{8,9},{9,8},{10,11... | collective-permute-start | bytes 3145736 | tf_op jit(solution)/shard_map/ppermute | solution.py:141
  46.8 5.5 %collective-permute-start.1 = (bf16[128,2048]{1,0:T(8,128)(2,1)S(1)}, bf16[128,2048]{1,0:T(8,128)(2,1)S(1)}, u32[]{:S(2)}, u32[]{:S(2)}) collective-permute-start(bf16[128,2048]{1,0:T(8,128)(2,1)S(1)} %bitcast.47), channel_id=1, source_target_pairs={{0,1},{1,0},{2,3},{3,2},{4,5},{5,4},{6,7},{7,6},{8,9},{9,8},{10,11... | collective-permute-start | bytes 1572872 | tf_op jit(solution)/shard_map/ppermute | solution.py:141
  56.1 13.5 %collective-permute-start.2 = (s16[8,8,2176]{2,1,0:T(8,128)(2,1)S(1)}, s16[8,8,2176]{2,1,0:T(8,128)(2,1)S(1)}, u32[]{:S(2)}, u32[]{:S(2)}) collective-permute-start(s16[8,8,2176]{2,1,0:T(8,128)(2,1)S(1)} %give.1), channel_id=1, source_target_pairs={{0,32},{1,481},{32,0},{33,65},{64,96},{65,33},{96,64},{97,129},{12... | collective-permute-start | bytes 835592 | tf_op jit(solution)/shard_map/ppermute | solution.py:300
  100.8 26.7 %all-to-all-start.3 = ((bf16[16,16,1024]{2,1,0:T(8,128)(2,1)}), bf16[16,16,1024]{2,1,0:T(8,128)(2,1)S(1)}, u32[]{:S(2)}, u32[]{:S(2)}) async-start(bf16[16,16,1024]{2,1,0:T(8,128)(2,1)} %merge.4), calls=%async_computation.3 | async-start | bytes 1048576 | tf_op jit(solution)/shard_map/all_to_all | solution.py:145
  129.8 11.6 %collective-permute-start.3 = (f32[256,1024]{1,0:T(8,128)S(1)}, f32[256,1024]{1,0:T(8,128)S(1)}, u32[]{:S(2)}, u32[]{:S(2)}) collective-permute-start(f32[256,1024]{1,0:T(8,128)S(1)} %fusion.7), channel_id=1, source_target_pairs={{0,1},{1,0},{2,3},{3,2},{4,5},{5,4},{6,7},{7,6},{8,9},{9,8},{10,11... | collective-permute-start | bytes 3145736 | tf_op jit(solution)/shard_map/ppermute | solution.py:141
  139.1 24.2 %copy-start.2 = (s32[6]{0:T(128)S(1)}, s32[6]{0:T(128)}, u32[]{:S(2)}) copy-start(s32[6]{0:T(128)} %param.9) | copy-start | bytes 76
  142.8 15.2 %all-to-all-start.4 = ((s16[16,8,2176]{2,1,0:T(8,128)(2,1)}), s16[16,8,2176]{2,1,0:T(8,128)(2,1)S(1)}, u32[]{:S(2)}, u32[]{:S(2)}) async-start(s16[16,8,2176]{2,1,0:T(8,128)(2,1)} %encode.3), calls=%async_computation.4 | async-start | bytes 1114112 | tf_op jit(solution)/shard_map/all_to_all | solution.py:145
  159.4 14.4 %all-to-all-start.5 = ((s16[16,8,2176]{2,1,0:T(8,128)(2,1)}), s16[16,8,2176]{2,1,0:T(8,128)(2,1)S(1)}, u32[]{:S(2)}, u32[]{:S(2)}) async-start(s16[16,8,2176]{2,1,0:T(8,128)(2,1)} %merge.5), calls=%async_computation.5 | async-start | bytes 1114112 | tf_op jit(solution)/shard_map/all_to_all | solution.py:145
  182.4 4.8 %collective-permute-start.4 = (s16[32,1152]{1,0:T(8,128)(2,1)S(1)}, s16[32,1152]{1,0:T(8,128)(2,1)S(1)}, u32[]{:S(2)}, u32[]{:S(2)}) collective-permute-start(s16[32,1152]{1,0:T(8,128)(2,1)S(1)} %get-tuple-element.19), channel_id=1, source_target_pairs={{0,1},{1,0},{2,3},{3,2},{4,5},{5,4},{6,7},{7,6},{8,9},{9,8},{10,11... | collective-permute-start | bytes 221192 | tf_op jit(solution)/shard_map/ppermute | solution.py:141
  194.0 5.1 %collective-permute-start.5 = (s16[32,1152]{1,0:T(8,128)(2,1)S(1)}, s16[32,1152]{1,0:T(8,128)(2,1)S(1)}, u32[]{:S(2)}, u32[]{:S(2)}) collective-permute-start(s16[32,1152]{1,0:T(8,128)(2,1)S(1)} %get-tuple-element.22), channel_id=1, source_target_pairs={{0,32},{32,0},{64,96},{96,64},{128,160},{160,128},{192,224},{224,1... | collective-permute-start | bytes 221192 | tf_op jit(solution)/shard_map/ppermute | solution.py:328
  205.8 6.8 %collective-permute-start.6 = (s16[32,1152]{1,0:T(8,128)(2,1)S(1)}, s16[32,1152]{1,0:T(8,128)(2,1)S(1)}, u32[]{:S(2)}, u32[]{:S(2)}) collective-permute-start(s16[32,1152]{1,0:T(8,128)(2,1)S(1)} %get-tuple-element.42), channel_id=1, source_target_pairs={{0,64},{32,96},{64,0},{96,32},{128,192},{160,224},{192,128},{224,1... | collective-permute-start | bytes 221192 | tf_op jit(solution)/shard_map/ppermute | solution.py:328
  219.4 10.6 %collective-permute-start.7 = (s16[32,1152]{1,0:T(8,128)(2,1)S(1)}, s16[32,1152]{1,0:T(8,128)(2,1)S(1)}, u32[]{:S(2)}, u32[]{:S(2)}) collective-permute-start(s16[32,1152]{1,0:T(8,128)(2,1)S(1)} %get-tuple-element.36), channel_id=1, source_target_pairs={{0,128},{32,160},{64,192},{96,224},{128,0},{160,32},{192,64},{224,... | collective-permute-start | bytes 221192 | tf_op jit(solution)/shard_map/ppermute | solution.py:328
  236.7 13.1 %collective-permute-start.8 = (f32[16,128]{1,0:T(8,128)S(1)}, f32[16,128]{1,0:T(8,128)S(1)}, u32[]{:S(2)}, u32[]{:S(2)}) collective-permute-start(f32[16,128]{1,0:T(8,128)S(1)} %constant_dynamic-slice_fusion), channel_id=1, source_target_pairs={{0,256},{32,288},{64,320},{96,352},{128,384},{160,416},{192,448},{... | collective-permute-start | bytes 24584 | tf_op jit(solution)/shard_map/ppermute | solution.py:332
  243.1 7.3 %copy-start.1 = (f32[5,128,256]{2,1,0:T(8,128)}, f32[5,128,256]{2,1,0:T(8,128)S(1)}, u32[]{:S(2)}) copy-start(f32[5,128,256]{2,1,0:T(8,128)S(1)} %broadcast_dynamic-update-slice_fusion) | copy-start | bytes 1966084

commit v4 on v3

--- a/solution.py
+++ b/solution.py
@@ -258,7 +258,6 @@
     rows, width = front.shape
     leaf_rows = rows // 2
     samples = sample.shape[0]
-    half = samples // 2
     top = sketch.shape[2]
     n_leaf = lax.axis_size("leaf")
     n_samp = lax.axis_size("samp")
@@ -270,25 +269,28 @@
     bf16 = jnp.bfloat16
 
     block = 2 * s + c
-    flags = lax.dynamic_slice(pattern, (2 * z, block), (2, 1))
-    leaf_mask = jnp.repeat(flags, leaf_rows, axis=0).reshape(1, rows)
-
-    def first_half(which):
-        part = lax.dynamic_slice_in_dim(sample, which * half, half, 0)
-        part = lax.dot_general(part, front, COLS, preferred_element_type=f32)
-        return part * leaf_mask.astype(f32)
-
-    away = swap_cores(first_half(1 - c))
-    message = packed([first_half(c), away], n_samp)
-    pieces = merged(exchange(message, "samp"), n_samp, half // n_samp, rows)
-    mine = exchange(pieces, "samp").reshape(half, rows)
+    flags = lax.dynamic_slice(pattern, (2 * z, block), (2, 1)).astype(f32)
+
+    def of_leaf(which):
+        part = lax.dynamic_slice_in_dim(front, which * leaf_rows, leaf_rows, 0)
+        return part, lax.dynamic_slice_in_dim(flags, which, 1, 0)
+
+    def onto_leaf(which, left):
+        part, flag = of_leaf(which)
+        return lax.dot_general(left, part, COLS, preferred_element_type=f32) * flag
+
+    def from_leaf(which, left):
+        part, flag = of_leaf(which)
+        return jnp.dot(left, part, preferred_element_type=f32) * flag
+
+    away = swap_cores(onto_leaf(1 - c, sample))
+    message = packed([onto_leaf(c, sample), away], n_samp)
+    share = samples // n_samp
+    pieces = merged(exchange(message, "samp"), n_samp, share, leaf_rows)
+    mine = exchange(pieces, "samp").reshape(samples, leaf_rows)
     other = swap_cores(mine)
-    first_sample = jnp.where(
-        c == 0, jnp.concatenate([mine, other], 0), jnp.concatenate([other, mine], 0)
-    )
-    first_sample = first_sample * leaf_mask.astype(bf16)
-
-    back_part = jnp.dot(first_sample, front, preferred_element_type=f32)
+
+    back_part = lax.optimization_barrier(from_leaf(c, mine)) + from_leaf(1 - c, other)
     parity = (z % 2).astype(jnp.int32).reshape(1)
     pairs = []
     for i in range(n_leaf):
@@ -303,13 +305,8 @@
     pieces = merged(exchange(message, "leaf", same), n_leaf, samples // n_leaf, width)
     back_sample = exchange(pieces, "leaf").reshape(samples, width)
 
-    def third_half(which):
-        part = lax.dynamic_slice_in_dim(front, which * leaf_rows, leaf_rows, 0)
-        flag = lax.dynamic_slice_in_dim(flags, which, 1, 0).astype(f32)
-        return lax.dot_general(back_sample, part, COLS, preferred_element_type=f32) * flag
-
-    away = swap_cores(third_half(1 - c))
-    message = packed([third_half(c), away], n_samp)
+    away = swap_cores(onto_leaf(1 - c, back_sample))
+    message = packed([onto_leaf(c, back_sample), away], n_samp)
     columns = exchange(merged_again(exchange(message, "samp"), n_samp), "samp")
 
     uppers = [c, c] + [z // 2**bit % 2 for bit in range(depth - 1)]
@@ -326,7 +323,6 @@
         if not last:
             pairs = [(i, i ^ (1 << (level - 1))) for i in range(n_leaf)]
             partner = lax.ppermute(message[0], "leaf", pairs)
-    share = samples // n_samp
     mine = lax.dynamic_slice_in_dim(reduced, s * share, share, 0)
     bit = depth - 1
     other = lax.ppermute(mine, "leaf", [(i, i ^ (1 << bit)) for i in range(n_leaf)])

time: 255 us -> 252 us (0.988)
  the two profiles are of different devices: /device:TPU:1 before, /device:TPU:2 now
where the time goes in v4:
time: 252 us; the launch traced here: 251 us
  blocking collectives  102 us (40%)
  waiting for transfers between devices  50.6 us (20%)
  starting transfers between devices  39.5 us (16%)
  local copies, waits for them, and re-layouts  21.1 us (8%)
  Pallas kernels  20.7 us (8%)
  matrix products  15.1 us (6%)
    all_to_all x4, blocking collectives, exchange(): return lax.all_to_all(x, axis, 0, 0, axis_index_groups=groups)  102 us
    all_to_all x2, waiting for transfers between devices, exchange(): return lax.all_to_all(x, axis, 0, 0, axis_index_groups=groups)  21 us
    pallas_call x3, local copies, waits for them, and re-layouts, compress(): pl.pallas_call(functools.partial(kernel, level), in_specs=[pl.BlockSpec(m...  20.2 us
    pallas_call x2, Pallas kernels, compress(): pl.pallas_call(functools.partial(kernel, level), in_specs=[pl.BlockSpec(m...  15.3 us
    ppermute x3, waiting for transfers between devices, body(): partner = lax.ppermute(message[0], 'leaf', pairs)  13.5 us
    ppermute x3, starting transfers between devices, body(): partner = lax.ppermute(message[0], 'leaf', pairs)  13.1 us
    all_to_all x2, starting transfers between devices, exchange(): return lax.all_to_all(x, axis, 0, 0, axis_index_groups=groups)  9.65 us
    dot_general x4, matrix products, onto_leaf(): return lax.dot_general(left, part, COLS, preferred_element_type=f32) * flag  8.84 us
  transfers between devices with their start and end apart: 11, of which 9 were waited for; matrix products, arithmetic and copies ran while one was open for 3% of the time, Pallas kernels for 0%

profile of v4, /device:TPU:2, one launch (start us, length us, event | category | flops | bytes accessed | tf_op | source)
XLA Modules:
  0.0 251.3 jit_solution(13475007634184203796)
XLA Ops:
  0.6 0.0 copy-start
  0.7 0.8 dynamic-slice_convert_fusion
  1.5 0.6 constant_dynamic-slice_fusion.1
  2.1 3.0 %fusion.27 = f32[256,1024]{1,0:T(8,128)S(1)} fusion(bf16[256,1024]{1,0:T(8,128)(2,1)S(1)} %copy-done, bf16[2048,1024]{1,0:T(8,128)(2,1)} %param.5, s32[]{:T(128)S(6)} %select_n.82, f32[]{:T(128)} %bitcast.8), kind=kOutput, calls=%fused_computation.17 | convolution fusion | flops 537133056 | bytes 3670532 | tf_op jit(solution)/shard_map/dot_general | solution.py:280
  5.1 1.9 collective-permute-start
  7.0 3.0 %fusion.15.refs_0_ = f32[256,1024]{1,0:T(8,128)S(1)} fusion(bf16[256,1024]{1,0:T(8,128)(2,1)S(1)} %copy-done, bf16[2048,1024]{1,0:T(8,128)(2,1)} %param.5, s32[]{:T(128)S(6)} %select_n.78, f32[]{:T(128)} %bitcast.6), kind=kOutput, calls=%fused_computation.13 | convolution fusion | flops 537133056 | bytes 3670532 | tf_op jit(solution)/shard_map/dot_general | solution.py:280
  10.0 0.5 encode.2
  10.6 20.0 %all_to_all.30.message_ref = s16[16,8,2176]{2,1,0:T(8,128)(2,1)S(1)} all-to-all(s16[16,8,2176]{2,1,0:T(8,128)(2,1)S(1)} %encode.2), channel_id=1, replica_groups=mesh['leaf'=16,'samp'=16,'cblk'=2] {'samp'}, dimensions={0} | all-to-all | bytes 1114112 | tf_op jit(solution)/shard_map/all_to_all | solution.py:145
  30.6 0.5 merge.3
  31.1 14.3 %all_to_all.31 = bf16[16,16,1024]{2,1,0:T(8,128)(2,1)S(1)} all-to-all(bf16[16,16,1024]{2,1,0:T(8,128)(2,1)S(1)} %merge.3), channel_id=1, replica_groups=mesh['leaf'=16,'samp'=16,'cblk'=2] {'samp'}, dimensions={0} | all-to-all | bytes 1048576 | tf_op jit(solution)/shard_map/all_to_all | solution.py:145
  45.4 1.9 collective-permute-start.1
  47.3 3.0 %fusion.18 = f32[256,1024]{1,0:T(8,128)S(1)} fusion(bf16[256,1024]{1,0:T(8,128)(2,1)S(1)} %bitcast.43, bf16[2048,1024]{1,0:T(8,128)(2,1)} %param.5, s32[]{:T(128)S(6)} %select_n.78, f32[]{:T(128)} %bitcast.6), kind=kOutput, calls=%fused_computation.14 | convolution fusion | flops 537133056 | bytes 3670532 | tf_op jit(solution)/shard_map/dot_general | solution.py:284
  50.4 3.3 %fusion.33.part_ref = f32[256,1024]{1,0:T(8,128)S(1)} fusion(f32[256,1024]{1,0:T(8,128)S(1)} %fusion.18, bf16[256,1024]{1,0:T(8,128)(2,1)S(1)} %collective-permute-done.1, bf16[2048,1024]{1,0:T(8,128)(2,1)} %param.5, s32[]{:T(128)S(6)} %select_n.82, f32[]{:T(128)} %bitcast.8), kind=kOutput, calls=%fused_computation.19 | convolution fusion | flops 537395200 | bytes 4719108 | tf_op jit(solution)/shard_map/dot_general | solution.py:284
  53.7 0.3 give.1
  54.0 2.2 collective-permute-start.2
  56.2 6.2 %collective-permute-done.2.message_ref = s16[8,8,2176]{2,1,0:T(8,128)(2,1)S(1)} collective-permute-done((s16[8,8,2176]{2,1,0:T(8,128)(2,1)S(1)}, s16[8,8,2176]{2,1,0:T(8,128)(2,1)S(1)}, u32[]{:S(2)}, u32[]{:S(2)}) %collective-permute-start.2) | collective-permute-done | bytes 278560 | tf_op jit(solution)/shard_map/ppermute | solution.py:302
  62.4 0.9 keep.1
  63.3 35.6 %all_to_all.32.message_ref = s16[8,8,2176]{2,1,0:T(8,128)(2,1)S(1)} all-to-all(s16[8,8,2176]{2,1,0:T(8,128)(2,1)S(1)} %keep.1), channel_id=1, replica_groups={{0,64,128,192,256,320,384,448},{32,96,160,224,288,352,416,480},{1,65,12..., dimensions={0} | all-to-all | bytes 557056 | tf_op jit(solution)/shard_map/all_to_all | solution.py:145
  98.9 0.3 merge.4
  99.2 31.9 %all_to_all.33 = bf16[16,16,1024]{2,1,0:T(8,128)(2,1)S(1)} all-to-all(bf16[16,16,1024]{2,1,0:T(8,128)(2,1)S(1)} %merge.4), channel_id=1, replica_groups=mesh['leaf'=16,'samp'=16,'cblk'=2] {'leaf'}, dimensions={0} | all-to-all | bytes 1048576 | tf_op jit(solution)/shard_map/all_to_all | solution.py:145
  131.1 1.4 fusion.36
  132.6 2.1 collective-permute-start.3
  134.6 1.4 fusion.21.refs_0_
  136.1 1.2 collective-permute-done.3.refs_1_
  137.3 1.4 encode.3
  138.6 4.8 %all-to-all-start.4 = ((s16[16,8,2176]{2,1,0:T(8,128)(2,1)}), s16[16,8,2176]{2,1,0:T(8,128)(2,1)S(1)}, u32[]{:S(2)}, u32[]{:S(2)}) async-start(s16[16,8,2176]{2,1,0:T(8,128)(2,1)} %encode.3), calls=%async_computation.4 | async-start | bytes 1114112 | tf_op jit(solution)/shard_map/all_to_all | solution.py:145
  143.4 0.1 stack.45
  143.5 11.1 %all-to-all-done.4.message_ref = s16[16,8,2176]{2,1,0:T(8,128)(2,1)S(1)} async-done(((s16[16,8,2176]{2,1,0:T(8,128)(2,1)}), s16[16,8,2176]{2,1,0:T(8,128)(2,1)S(1)}, u32[]{:S(2)}, u32[]{:S(2)}) %all-to-all-start.4) | async-done | bytes 557088 | tf_op jit(solution)/shard_map/all_to_all | solution.py:145
  154.6 1.4 merge.5
  156.1 4.8 %all-to-all-start.5 = ((s16[16,8,2176]{2,1,0:T(8,128)(2,1)}), s16[16,8,2176]{2,1,0:T(8,128)(2,1)S(1)}, u32[]{:S(2)}, u32[]{:S(2)}) async-start(s16[16,8,2176]{2,1,0:T(8,128)(2,1)} %merge.5), calls=%async_computation.5 | async-start | bytes 1114112 | tf_op jit(solution)/shard_map/all_to_all | solution.py:145
  160.9 0.1 copy.14.table_ref
  161.1 9.9 %all-to-all-done.5.columns_ref = s16[16,8,2176]{2,1,0:T(8,128)(2,1)S(1)} async-done(((s16[16,8,2176]{2,1,0:T(8,128)(2,1)}), s16[16,8,2176]{2,1,0:T(8,128)(2,1)S(1)}, u32[]{:S(2)}, u32[]{:S(2)}) %all-to-all-start.5) | async-done | bytes 557088 | tf_op jit(solution)/shard_map/all_to_all | solution.py:145
  170.9 8.6 %compress_leaf.1 = (f32[128,1024]{1,0:T(8,128)}, f32[256,128]{1,0:T(8,128)S(1)}, s16[32,1152]{1,0:T(8,128)(2,1)S(1)}) custom-call(s32[5,2]{1,0:T(8,128)S(1)} %copy.14.table_ref, s16[16,8,2176]{2,1,0:T(8,128)(2,1)S(1)} %all-to-all-done.5.columns_ref, f32[256,128]{1,0:T(8,128)S(1)} %get-tuple-element.50.weights_ref), custom_call_target="tpu_custom_call" | custom-call | tf_op jit(solution)/shard_map/compress_leaf/pallas_call | solution.py:130
  179.5 1.9 collective-permute-start.4
  181.4 1.2 collective-permute-done.4.other_ref
  182.6 6.8 %compress_node.4 = (f32[128,256]{1,0:T(8,128)S(1)}, f32[256,128]{1,0:T(8,128)S(1)}, s16[32,1152]{1,0:T(8,128)(2,1)S(1)}) custom-call(s32[5,2]{1,0:T(8,128)S(1)} %copy.14.table_ref, f32[256,128]{1,0:T(8,128)S(1)} %get-tuple-element.18.mine_ref, s16[32,1152]{1,0:T(8,128)(2,1)S(1)} %collective-permute-done.4.other_ref, f32[256,128]{1,0:T(8,128)S(1)} %get-tuple-element.49.weights_ref), custom_call_target="tpu_custom_call" | custom-call | tf_op jit(solution)/shard_map/compress_node/pallas_call | solution.py:130
  189.4 3.6 %collective-permute-start.5 = (s16[32,1152]{1,0:T(8,128)(2,1)S(1)}, s16[32,1152]{1,0:T(8,128)(2,1)S(1)}, u32[]{:S(2)}, u32[]{:S(2)}) collective-permute-start(s16[32,1152]{1,0:T(8,128)(2,1)S(1)} %get-tuple-element.22), channel_id=1, source_target_pairs={{0,32},{32,0},{64,96},{96,64},{128,160},{160,128},{192,224},{224,1... | collective-permute-start | bytes 221192 | tf_op jit(solution)/shard_map/ppermute | solution.py:325
  193.0 2.7 %collective-permute-done.5 = s16[32,1152]{1,0:T(8,128)(2,1)S(1)} collective-permute-done((s16[32,1152]{1,0:T(8,128)(2,1)S(1)}, s16[32,1152]{1,0:T(8,128)(2,1)S(1)}, u32[]{:S(2)}, u32[]{:S(2)}) %collective-permute-start.5) | collective-permute-done | bytes 73760 | tf_op jit(solution)/shard_map/ppermute | solution.py:325
  195.7 6.8 %compress_node.7 = (f32[5,128,256]{2,1,0:T(8,128)S(1)}, f32[256,128]{1,0:T(8,128)S(1)}, s16[32,1152]{1,0:T(8,128)(2,1)S(1)}) fusion(f32[5,128,256]{2,1,0:T(8,128)S(1)} %bitcast_dynamic-update-slice_fusion.3, s32[5,2]{1,0:T(8,128)S(1)} %copy.14.table_ref, f32[256,128]{1,0:T(8,128)S(1)} %get-tuple-element.21, s16[32,1152]{1,0:T(8,128)(2,1)S(1)} %collective-permute-done.5, ...), kind=kCustom, calls=%fused_computation.23 | custom fusion | bytes 675840 | tf_op jit(solution)/shard_map/compress_node/pallas_call | solution.py:130
  202.5 4.0 %collective-permute-start.6 = (s16[32,1152]{1,0:T(8,128)(2,1)S(1)}, s16[32,1152]{1,0:T(8,128)(2,1)S(1)}, u32[]{:S(2)}, u32[]{:S(2)}) collective-permute-start(s16[32,1152]{1,0:T(8,128)(2,1)S(1)} %get-tuple-element.40), channel_id=1, source_target_pairs={{0,64},{32,96},{64,0},{96,32},{128,192},{160,224},{192,128},{224,1... | collective-permute-start | bytes 221192 | tf_op jit(solution)/shard_map/ppermute | solution.py:325
  206.5 3.1 %collective-permute-done.6 = s16[32,1152]{1,0:T(8,128)(2,1)S(1)} collective-permute-done((s16[32,1152]{1,0:T(8,128)(2,1)S(1)}, s16[32,1152]{1,0:T(8,128)(2,1)S(1)}, u32[]{:S(2)}, u32[]{:S(2)}) %collective-permute-start.6) | collective-permute-done | bytes 73760 | tf_op jit(solution)/shard_map/ppermute | solution.py:325
  209.6 6.8 %compress_node.6 = (f32[5,128,256]{2,1,0:T(8,128)S(1)}, f32[256,128]{1,0:T(8,128)S(1)}, s16[32,1152]{1,0:T(8,128)(2,1)S(1)}) fusion(f32[5,128,256]{2,1,0:T(8,128)S(1)} %get-tuple-element.37, s32[5,2]{1,0:T(8,128)S(1)} %copy.14.table_ref, f32[256,128]{1,0:T(8,128)S(1)} %get-tuple-element.38, s16[32,1152]{1,0:T(8,128)(2,1)S(1)} %collective-permute-done.6, ...), kind=kCustom, calls=%fused_computation.22 | custom fusion | bytes 675840 | tf_op jit(solution)/shard_map/compress_node/pallas_call | solution.py:130
  216.4 5.6 %collective-permute-start.7 = (s16[32,1152]{1,0:T(8,128)(2,1)S(1)}, s16[32,1152]{1,0:T(8,128)(2,1)S(1)}, u32[]{:S(2)}, u32[]{:S(2)}) collective-permute-start(s16[32,1152]{1,0:T(8,128)(2,1)S(1)} %get-tuple-element.46), channel_id=1, source_target_pairs={{0,128},{32,160},{64,192},{96,224},{128,0},{160,32},{192,64},{224,... | collective-permute-start | bytes 221192 | tf_op jit(solution)/shard_map/ppermute | solution.py:325
  222.0 7.7 %collective-permute-done.7 = s16[32,1152]{1,0:T(8,128)(2,1)S(1)} collective-permute-done((s16[32,1152]{1,0:T(8,128)(2,1)S(1)}, s16[32,1152]{1,0:T(8,128)(2,1)S(1)}, u32[]{:S(2)}, u32[]{:S(2)}) %collective-permute-start.7) | collective-permute-done | bytes 73760 | tf_op jit(solution)/shard_map/ppermute | solution.py:325
  229.7 6.7 %compress_node.5 = (f32[5,128,256]{2,1,0:T(8,128)S(1)}, f32[256,128]{1,0:T(8,128)S(1)}) fusion(f32[5,128,256]{2,1,0:T(8,128)S(1)} %get-tuple-element.43, s32[5,2]{1,0:T(8,128)S(1)} %copy.14.table_ref, f32[256,128]{1,0:T(8,128)S(1)} %get-tuple-element.44, s16[32,1152]{1,0:T(8,128)(2,1)S(1)} %collective-permute-done.7, f32[256,128]{1,0:T(8,128)S(1)} %get-tuple-element.47), kind=kCustom, calls=%fused_computation.21 | custom fusion | bytes 602112 | tf_op jit(solution)/shard_map/compress_node/pallas_call | solution.py:130
  236.4 6.7 %collective-permute-start.8 = (f32[16,128]{1,0:T(8,128)S(1)}, f32[16,128]{1,0:T(8,128)S(1)}, u32[]{:S(2)}, u32[]{:S(2)}) collective-permute-start(f32[16,128]{1,0:T(8,128)S(1)} %constant_dynamic-slice_fusion), channel_id=1, source_target_pairs={{0,256},{32,288},{64,320},{96,352},{128,384},{160,416},{192,448},{... | collective-permute-start | bytes 24584 | tf_op jit(solution)/shard_map/ppermute | solution.py:328
  243.1 7.5 %collective-permute-done.8 = f32[16,128]{1,0:T(8,128)S(1)} collective-permute-done((f32[16,128]{1,0:T(8,128)S(1)}, f32[16,128]{1,0:T(8,128)S(1)}, u32[]{:S(2)}, u32[]{:S(2)}) %collective-permute-start.8) | collective-permute-done | bytes 8224 | tf_op jit(solution)/shard_map/ppermute | solution.py:328
  250.6 0.6 pad_maximum_fusion
  (18 shorter events, 0.1 us)
Async XLA Ops:
  0.6 1.5 copy-start
  5.1 5.0 %collective-permute-start = (f32[256,1024]{1,0:T(8,128)S(1)}, f32[256,1024]{1,0:T(8,128)S(1)}, u32[]{:S(2)}, u32[]{:S(2)}) collective-permute-start(f32[256,1024]{1,0:T(8,128)S(1)} %fusion.27), channel_id=1, source_target_pairs={{0,1},{1,0},{2,3},{3,2},{4,5},{5,4},{6,7},{7,6},{8,9},{9,8},{10,11... | collective-permute-start | bytes 3145736 | tf_op jit(solution)/shard_map/ppermute | solution.py:141
  45.4 4.9 %collective-permute-start.1 = (bf16[256,1024]{1,0:T(8,128)(2,1)S(1)}, bf16[256,1024]{1,0:T(8,128)(2,1)S(1)}, u32[]{:S(2)}, u32[]{:S(2)}) collective-permute-start(bf16[256,1024]{1,0:T(8,128)(2,1)S(1)} %bitcast.42), channel_id=1, source_target_pairs={{0,1},{1,0},{2,3},{3,2},{4,5},{5,4},{6,7},{7,6},{8,9},{9,8},{10,11... | collective-permute-start | bytes 1572872 | tf_op jit(solution)/shard_map/ppermute | solution.py:141
  50.3 80.8 %copy-start.1 = (bf16[2048,1024]{1,0:T(8,128)(2,1)S(1)}, bf16[2048,1024]{1,0:T(8,128)(2,1)}, u32[]{:S(2)}) copy-start(bf16[2048,1024]{1,0:T(8,128)(2,1)} %param.5) | copy-start | bytes 12582916
  54.0 8.4 %collective-permute-start.2 = (s16[8,8,2176]{2,1,0:T(8,128)(2,1)S(1)}, s16[8,8,2176]{2,1,0:T(8,128)(2,1)S(1)}, u32[]{:S(2)}, u32[]{:S(2)}) collective-permute-start(s16[8,8,2176]{2,1,0:T(8,128)(2,1)S(1)} %give.1), channel_id=1, source_target_pairs={{0,32},{1,481},{32,0},{33,65},{64,96},{65,33},{96,64},{97,129},{12... | collective-permute-start | bytes 835592 | tf_op jit(solution)/shard_map/ppermute | solution.py:302
  132.6 28.4 %copy-start.4 = (s32[6]{0:T(128)S(1)}, s32[6]{0:T(128)}, u32[]{:S(2)}) copy-start(s32[6]{0:T(128)} %param.9) | copy-start | bytes 76
  132.6 28.5 %copy-start.2 = (f32[6,256,128]{2,1,0:T(8,128)S(1)}, f32[6,256,128]{2,1,0:T(8,128)}, u32[]{:S(2)}) copy-start(f32[6,256,128]{2,1,0:T(8,128)} %param.8) | copy-start | bytes 2359300
  132.6 4.7 %collective-permute-start.3 = (f32[256,1024]{1,0:T(8,128)S(1)}, f32[256,1024]{1,0:T(8,128)S(1)}, u32[]{:S(2)}, u32[]{:S(2)}) collective-permute-start(f32[256,1024]{1,0:T(8,128)S(1)} %fusion.36), channel_id=1, source_target_pairs={{0,1},{1,0},{2,3},{3,2},{4,5},{5,4},{6,7},{7,6},{8,9},{9,8},{10,11... | collective-permute-start | bytes 3145736 | tf_op jit(solution)/shard_map/ppermute | solution.py:141
  138.6 16.0 %all-to-all-start.4 = ((s16[16,8,2176]{2,1,0:T(8,128)(2,1)}), s16[16,8,2176]{2,1,0:T(8,128)(2,1)S(1)}, u32[]{:S(2)}, u32[]{:S(2)}) async-start(s16[16,8,2176]{2,1,0:T(8,128)(2,1)} %encode.3), calls=%async_computation.4 | async-start | bytes 1114112 | tf_op jit(solution)/shard_map/all_to_all | solution.py:145
  156.1 14.9 %all-to-all-start.5 = ((s16[16,8,2176]{2,1,0:T(8,128)(2,1)}), s16[16,8,2176]{2,1,0:T(8,128)(2,1)S(1)}, u32[]{:S(2)}, u32[]{:S(2)}) async-start(s16[16,8,2176]{2,1,0:T(8,128)(2,1)} %merge.5), calls=%async_computation.5 | async-start | bytes 1114112 | tf_op jit(solution)/shard_map/all_to_all | solution.py:145
  179.5 3.1 %collective-permute-start.4 = (s16[32,1152]{1,0:T(8,128)(2,1)S(1)}, s16[32,1152]{1,0:T(8,128)(2,1)S(1)}, u32[]{:S(2)}, u32[]{:S(2)}) collective-permute-start(s16[32,1152]{1,0:T(8,128)(2,1)S(1)} %get-tuple-element.19), channel_id=1, source_target_pairs={{0,1},{1,0},{2,3},{3,2},{4,5},{5,4},{6,7},{7,6},{8,9},{9,8},{10,11... | collective-permute-start | bytes 221192 | tf_op jit(solution)/shard_map/ppermute | solution.py:141
  189.4 6.2 %collective-permute-start.5 = (s16[32,1152]{1,0:T(8,128)(2,1)S(1)}, s16[32,1152]{1,0:T(8,128)(2,1)S(1)}, u32[]{:S(2)}, u32[]{:S(2)}) collective-permute-start(s16[32,1152]{1,0:T(8,128)(2,1)S(1)} %get-tuple-element.22), channel_id=1, source_target_pairs={{0,32},{32,0},{64,96},{96,64},{128,160},{160,128},{192,224},{224,1... | collective-permute-start | bytes 221192 | tf_op jit(solution)/shard_map/ppermute | solution.py:325
  202.5 7.1 %collective-permute-start.6 = (s16[32,1152]{1,0:T(8,128)(2,1)S(1)}, s16[32,1152]{1,0:T(8,128)(2,1)S(1)}, u32[]{:S(2)}, u32[]{:S(2)}) collective-permute-start(s16[32,1152]{1,0:T(8,128)(2,1)S(1)} %get-tuple-element.40), channel_id=1, source_target_pairs={{0,64},{32,96},{64,0},{96,32},{128,192},{160,224},{192,128},{224,1... | collective-permute-start | bytes 221192 | tf_op jit(solution)/shard_map/ppermute | solution.py:325
  216.4 13.3 %collective-permute-start.7 = (s16[32,1152]{1,0:T(8,128)(2,1)S(1)}, s16[32,1152]{1,0:T(8,128)(2,1)S(1)}, u32[]{:S(2)}, u32[]{:S(2)}) collective-permute-start(s16[32,1152]{1,0:T(8,128)(2,1)S(1)} %get-tuple-element.46), channel_id=1, source_target_pairs={{0,128},{32,160},{64,192},{96,224},{128,0},{160,32},{192,64},{224,... | collective-permute-start | bytes 221192 | tf_op jit(solution)/shard_map/ppermute | solution.py:325
  236.4 14.3 %collective-permute-start.8 = (f32[16,128]{1,0:T(8,128)S(1)}, f32[16,128]{1,0:T(8,128)S(1)}, u32[]{:S(2)}, u32[]{:S(2)}) collective-permute-start(f32[16,128]{1,0:T(8,128)S(1)} %constant_dynamic-slice_fusion), channel_id=1, source_target_pairs={{0,256},{32,288},{64,320},{96,352},{128,384},{160,416},{192,448},{... | collective-permute-start | bytes 24584 | tf_op jit(solution)/shard_map/ppermute | solution.py:328
  243.1 8.1 %copy-start.3 = (f32[5,128,256]{2,1,0:T(8,128)}, f32[5,128,256]{2,1,0:T(8,128)S(1)}, u32[]{:S(2)}) copy-start(f32[5,128,256]{2,1,0:T(8,128)S(1)} %broadcast_dynamic-update-slice_fusion) | copy-start | bytes 1966084

commit v5 on v4

--- a/solution.py
+++ b/solution.py
@@ -57,10 +57,20 @@
         if b + 1 < count:
             scaled = panel * inverse
             outside = (lane < start) | (lane >= stop)
-            update = exact_dot(scaled[:, stop:], panel, ROWS)
-            for i in range(b + 1, count):
-                at = ROW_BLOCK * (i - b - 1)
-                panels[i] = jnp.where(outside, panels[i], 0.0) - update[at : at + ROW_BLOCK, :]
+            column = jnp.transpose(scaled)[stop : stop + ROW_BLOCK, :]
+            terms = [
+                jnp.broadcast_to(column[:, k : k + 1], (ROW_BLOCK, n))
+                * jnp.broadcast_to(panel[k : k + 1, :], (ROW_BLOCK, n))
+                for k in range(ROW_BLOCK)
+            ]
+            while len(terms) > 1:
+                terms = [terms[i] + terms[i + 1] for i in range(0, len(terms), 2)]
+            panels[b + 1] = jnp.where(outside, panels[b + 1], 0.0) - terms[0]
+            if b + 2 < count:
+                update = exact_dot(scaled[:, stop + ROW_BLOCK :], panel, ROWS)
+                for i in range(b + 2, count):
+                    at = ROW_BLOCK * (i - b - 2)
+                    panels[i] = jnp.where(outside, panels[i], 0.0) - update[at : at + ROW_BLOCK, :]
     return jnp.concatenate(finished, axis=0)
 
 
@@ -325,7 +335,7 @@
             partner = lax.ppermute(message[0], "leaf", pairs)
     mine = lax.dynamic_slice_in_dim(reduced, s * share, share, 0)
     bit = depth - 1
-    other = lax.ppermute(mine, "leaf", [(i, i ^ (1 << bit)) for i in range(n_leaf)])
+    other = lax.ppermute(mine, "leaf", [(i, n_leaf - 1 - i) for i in range(n_leaf)])
     upper = z // 2**bit % 2 == 1
     root = jnp.concatenate([jnp.where(upper, other, mine), jnp.where(upper, mine, other)], axis=1)
     empty = jnp.zeros((top, 2 * top), f32)

time: 252 us -> 244 us (0.968)
  the two profiles are of different devices: /device:TPU:2 before, /device:TPU:1 now
where the time goes in v5:
time: 244 us; the launch traced here: 243 us
  blocking collectives  83.2 us (34%)
  starting transfers between devices  69.2 us (28%)
  waiting for transfers between devices  33.5 us (14%)
  local copies, waits for them, and re-layouts  19.6 us (8%)
  Pallas kernels  19.4 us (8%)
  matrix products  15.1 us (6%)
    all_to_all x4, blocking collectives, exchange(): return lax.all_to_all(x, axis, 0, 0, axis_index_groups=groups)  83.2 us
    ppermute x4, starting transfers between devices, swap_cores(): return lax.ppermute(x, 'cblk', [(0, 1), (1, 0)])  26.1 us
    all_to_all x2, waiting for transfers between devices, exchange(): return lax.all_to_all(x, axis, 0, 0, axis_index_groups=groups)  21.2 us
    pallas_call x3, local copies, waits for them, and re-layouts, compress(): pl.pallas_call(functools.partial(kernel, level), in_specs=[pl.BlockSpec(m...  18.7 us
    ppermute x3, starting transfers between devices, body(): partner = lax.ppermute(message[0], 'leaf', pairs)  14.4 us
    pallas_call x2, Pallas kernels, compress(): pl.pallas_call(functools.partial(kernel, level), in_specs=[pl.BlockSpec(m...  14 us
    ppermute x1, starting transfers between devices, body(): lax.ppermute(mine, 'leaf', [(i, n_leaf - 1 - i) for i in range(n_leaf)])  12 us
    ppermute x1, starting transfers between devices, body(): given = lax.ppermute(given, ('leaf', 'cblk'), pairs)  9.53 us
  transfers between devices with their start and end apart: 11, of which 9 were waited for; matrix products, arithmetic and copies ran while one was open for 3% of the time, Pallas kernels for 0%

profile of v5, /device:TPU:1, one launch (start us, length us, event | category | flops | bytes accessed | tf_op | source)
XLA Modules:
  0.0 242.7 jit_solution(1639021625691487731)
XLA Ops:
  0.6 0.0 copy-start
  0.7 0.8 dynamic-slice_convert_fusion
  1.5 0.6 constant_dynamic-slice_fusion.1
  2.1 3.0 %fusion.27 = f32[256,1024]{1,0:T(8,128)S(1)} fusion(bf16[256,1024]{1,0:T(8,128)(2,1)S(1)} %copy-done, bf16[2048,1024]{1,0:T(8,128)(2,1)} %param.5, s32[]{:T(128)S(6)} %select_n.82, f32[]{:T(128)} %bitcast.8), kind=kOutput, calls=%fused_computation.17 | convolution fusion | flops 537133056 | bytes 3670532 | tf_op jit(solution)/shard_map/dot_general | solution.py:290
  5.1 8.7 %collective-permute-start = (f32[256,1024]{1,0:T(8,128)S(1)}, f32[256,1024]{1,0:T(8,128)S(1)}, u32[]{:S(2)}, u32[]{:S(2)}) collective-permute-start(f32[256,1024]{1,0:T(8,128)S(1)} %fusion.27), channel_id=1, source_target_pairs={{0,1},{1,0},{2,3},{3,2},{4,5},{5,4},{6,7},{7,6},{8,9},{9,8},{10,11... | collective-permute-start | bytes 3145736 | tf_op jit(solution)/shard_map/ppermute | solution.py:151
  13.8 3.0 %fusion.15.refs_0_ = f32[256,1024]{1,0:T(8,128)S(1)} fusion(bf16[256,1024]{1,0:T(8,128)(2,1)S(1)} %copy-done, bf16[2048,1024]{1,0:T(8,128)(2,1)} %param.5, s32[]{:T(128)S(6)} %select_n.78, f32[]{:T(128)} %bitcast.6), kind=kOutput, calls=%fused_computation.13 | convolution fusion | flops 537133056 | bytes 3670532 | tf_op jit(solution)/shard_map/dot_general | solution.py:290
  16.9 0.5 encode.2
  17.4 14.6 %all_to_all.30.message_ref = s16[16,8,2176]{2,1,0:T(8,128)(2,1)S(1)} all-to-all(s16[16,8,2176]{2,1,0:T(8,128)(2,1)S(1)} %encode.2), channel_id=1, replica_groups=mesh['leaf'=16,'samp'=16,'cblk'=2] {'samp'}, dimensions={0} | all-to-all | bytes 1114112 | tf_op jit(solution)/shard_map/all_to_all | solution.py:155
  32.0 0.5 merge.3
  32.6 13.2 %all_to_all.31 = bf16[16,16,1024]{2,1,0:T(8,128)(2,1)S(1)} all-to-all(bf16[16,16,1024]{2,1,0:T(8,128)(2,1)S(1)} %merge.3), channel_id=1, replica_groups=mesh['leaf'=16,'samp'=16,'cblk'=2] {'samp'}, dimensions={0} | all-to-all | bytes 1048576 | tf_op jit(solution)/shard_map/all_to_all | solution.py:155
  45.7 4.0 %collective-permute-start.1 = (bf16[256,1024]{1,0:T(8,128)(2,1)S(1)}, bf16[256,1024]{1,0:T(8,128)(2,1)S(1)}, u32[]{:S(2)}, u32[]{:S(2)}) collective-permute-start(bf16[256,1024]{1,0:T(8,128)(2,1)S(1)} %bitcast.42), channel_id=1, source_target_pairs={{0,1},{1,0},{2,3},{3,2},{4,5},{5,4},{6,7},{7,6},{8,9},{9,8},{10,11... | collective-permute-start | bytes 1572872 | tf_op jit(solution)/shard_map/ppermute | solution.py:151
  49.7 3.0 %fusion.18 = f32[256,1024]{1,0:T(8,128)S(1)} fusion(bf16[256,1024]{1,0:T(8,128)(2,1)S(1)} %bitcast.43, bf16[2048,1024]{1,0:T(8,128)(2,1)} %param.5, s32[]{:T(128)S(6)} %select_n.78, f32[]{:T(128)} %bitcast.6), kind=kOutput, calls=%fused_computation.14 | convolution fusion | flops 537133056 | bytes 3670532 | tf_op jit(solution)/shard_map/dot_general | solution.py:294
  52.8 3.3 %fusion.33.part_ref = f32[256,1024]{1,0:T(8,128)S(1)} fusion(f32[256,1024]{1,0:T(8,128)S(1)} %fusion.18, bf16[256,1024]{1,0:T(8,128)(2,1)S(1)} %collective-permute-done.1, bf16[2048,1024]{1,0:T(8,128)(2,1)} %param.5, s32[]{:T(128)S(6)} %select_n.82, f32[]{:T(128)} %bitcast.8), kind=kOutput, calls=%fused_computation.19 | convolution fusion | flops 537395200 | bytes 4719108 | tf_op jit(solution)/shard_map/dot_general | solution.py:294
  56.1 0.3 give.1
  56.4 9.5 %collective-permute-start.2 = (s16[8,8,2176]{2,1,0:T(8,128)(2,1)S(1)}, s16[8,8,2176]{2,1,0:T(8,128)(2,1)S(1)}, u32[]{:S(2)}, u32[]{:S(2)}) collective-permute-start(s16[8,8,2176]{2,1,0:T(8,128)(2,1)S(1)} %give.1), channel_id=1, source_target_pairs={{0,32},{1,481},{32,0},{33,65},{64,96},{65,33},{96,64},{97,129},{12... | collective-permute-start | bytes 835592 | tf_op jit(solution)/shard_map/ppermute | solution.py:312
  65.9 3.9 %collective-permute-done.2.message_ref = s16[8,8,2176]{2,1,0:T(8,128)(2,1)S(1)} collective-permute-done((s16[8,8,2176]{2,1,0:T(8,128)(2,1)S(1)}, s16[8,8,2176]{2,1,0:T(8,128)(2,1)S(1)}, u32[]{:S(2)}, u32[]{:S(2)}) %collective-permute-start.2) | collective-permute-done | bytes 278560 | tf_op jit(solution)/shard_map/ppermute | solution.py:312
  69.8 0.9 keep.1
  70.7 29.5 %all_to_all.32.message_ref = s16[8,8,2176]{2,1,0:T(8,128)(2,1)S(1)} all-to-all(s16[8,8,2176]{2,1,0:T(8,128)(2,1)S(1)} %keep.1), channel_id=1, replica_groups={{0,64,128,192,256,320,384,448},{32,96,160,224,288,352,416,480},{1,65,12..., dimensions={0} | all-to-all | bytes 557056 | tf_op jit(solution)/shard_map/all_to_all | solution.py:155
  100.3 0.3 merge.4
  100.6 25.9 %all_to_all.33 = bf16[16,16,1024]{2,1,0:T(8,128)(2,1)S(1)} all-to-all(bf16[16,16,1024]{2,1,0:T(8,128)(2,1)S(1)} %merge.4), channel_id=1, replica_groups=mesh['leaf'=16,'samp'=16,'cblk'=2] {'leaf'}, dimensions={0} | all-to-all | bytes 1048576 | tf_op jit(solution)/shard_map/all_to_all | solution.py:155
  126.5 1.4 fusion.36
  128.0 9.1 %collective-permute-start.3 = (f32[256,1024]{1,0:T(8,128)S(1)}, f32[256,1024]{1,0:T(8,128)S(1)}, u32[]{:S(2)}, u32[]{:S(2)}) collective-permute-start(f32[256,1024]{1,0:T(8,128)S(1)} %fusion.36), channel_id=1, source_target_pairs={{0,1},{1,0},{2,3},{3,2},{4,5},{5,4},{6,7},{7,6},{8,9},{9,8},{10,11... | collective-permute-start | bytes 3145736 | tf_op jit(solution)/shard_map/ppermute | solution.py:151
  137.0 1.4 fusion.21.refs_0_
  138.5 0.8 collective-permute-done.3.refs_1_
  139.3 1.4 encode.3
  140.7 3.6 %all-to-all-start.4 = ((s16[16,8,2176]{2,1,0:T(8,128)(2,1)}), s16[16,8,2176]{2,1,0:T(8,128)(2,1)S(1)}, u32[]{:S(2)}, u32[]{:S(2)}) async-start(s16[16,8,2176]{2,1,0:T(8,128)(2,1)} %encode.3), calls=%async_computation.4 | async-start | bytes 1114112 | tf_op jit(solution)/shard_map/all_to_all | solution.py:155
  144.3 0.1 stack.45
  144.4 11.1 %all-to-all-done.4.message_ref = s16[16,8,2176]{2,1,0:T(8,128)(2,1)S(1)} async-done(((s16[16,8,2176]{2,1,0:T(8,128)(2,1)}), s16[16,8,2176]{2,1,0:T(8,128)(2,1)S(1)}, u32[]{:S(2)}, u32[]{:S(2)}) %all-to-all-start.4) | async-done | bytes 557088 | tf_op jit(solution)/shard_map/all_to_all | solution.py:155
  155.5 1.4 merge.5
  157.0 3.8 %all-to-all-start.5 = ((s16[16,8,2176]{2,1,0:T(8,128)(2,1)}), s16[16,8,2176]{2,1,0:T(8,128)(2,1)S(1)}, u32[]{:S(2)}, u32[]{:S(2)}) async-start(s16[16,8,2176]{2,1,0:T(8,128)(2,1)} %merge.5), calls=%async_computation.5 | async-start | bytes 1114112 | tf_op jit(solution)/shard_map/all_to_all | solution.py:155
  160.8 0.1 copy.14.table_ref
  160.9 10.1 %all-to-all-done.5.columns_ref = s16[16,8,2176]{2,1,0:T(8,128)(2,1)S(1)} async-done(((s16[16,8,2176]{2,1,0:T(8,128)(2,1)}), s16[16,8,2176]{2,1,0:T(8,128)(2,1)S(1)}, u32[]{:S(2)}, u32[]{:S(2)}) %all-to-all-start.5) | async-done | bytes 557088 | tf_op jit(solution)/shard_map/all_to_all | solution.py:155
  171.0 7.7 %compress_leaf.1 = (f32[128,1024]{1,0:T(8,128)}, f32[256,128]{1,0:T(8,128)S(1)}, s16[32,1152]{1,0:T(8,128)(2,1)S(1)}) custom-call(s32[5,2]{1,0:T(8,128)S(1)} %copy.14.table_ref, s16[16,8,2176]{2,1,0:T(8,128)(2,1)S(1)} %all-to-all-done.5.columns_ref, f32[256,128]{1,0:T(8,128)S(1)} %get-tuple-element.50.weights_ref), custom_call_target="tpu_custom_call" | custom-call | tf_op jit(solution)/shard_map/compress_leaf/pallas_call | solution.py:140
  178.7 4.2 %collective-permute-start.4 = (s16[32,1152]{1,0:T(8,128)(2,1)S(1)}, s16[32,1152]{1,0:T(8,128)(2,1)S(1)}, u32[]{:S(2)}, u32[]{:S(2)}) collective-permute-start(s16[32,1152]{1,0:T(8,128)(2,1)S(1)} %get-tuple-element.19), channel_id=1, source_target_pairs={{0,1},{1,0},{2,3},{3,2},{4,5},{5,4},{6,7},{7,6},{8,9},{9,8},{10,11... | collective-permute-start | bytes 221192 | tf_op jit(solution)/shard_map/ppermute | solution.py:151
  183.0 0.9 collective-permute-done.4.other_ref
  183.9 6.3 %compress_node.4 = (f32[128,256]{1,0:T(8,128)S(1)}, f32[256,128]{1,0:T(8,128)S(1)}, s16[32,1152]{1,0:T(8,128)(2,1)S(1)}) custom-call(s32[5,2]{1,0:T(8,128)S(1)} %copy.14.table_ref, f32[256,128]{1,0:T(8,128)S(1)} %get-tuple-element.18.mine_ref, s16[32,1152]{1,0:T(8,128)(2,1)S(1)} %collective-permute-done.4.other_ref, f32[256,128]{1,0:T(8,128)S(1)} %get-tuple-element.49.weights_ref), custom_call_target="tpu_custom_call" | custom-call | tf_op jit(solution)/shard_map/compress_node/pallas_call | solution.py:140
  190.2 3.5 %collective-permute-start.5 = (s16[32,1152]{1,0:T(8,128)(2,1)S(1)}, s16[32,1152]{1,0:T(8,128)(2,1)S(1)}, u32[]{:S(2)}, u32[]{:S(2)}) collective-permute-start(s16[32,1152]{1,0:T(8,128)(2,1)S(1)} %get-tuple-element.22), channel_id=1, source_target_pairs={{0,32},{32,0},{64,96},{96,64},{128,160},{160,128},{192,224},{224,1... | collective-permute-start | bytes 221192 | tf_op jit(solution)/shard_map/ppermute | solution.py:335
  193.7 1.6 collective-permute-done.5
  195.3 6.3 %compress_node.7 = (f32[5,128,256]{2,1,0:T(8,128)S(1)}, f32[256,128]{1,0:T(8,128)S(1)}, s16[32,1152]{1,0:T(8,128)(2,1)S(1)}) fusion(f32[5,128,256]{2,1,0:T(8,128)S(1)} %bitcast_dynamic-update-slice_fusion.3, s32[5,2]{1,0:T(8,128)S(1)} %copy.14.table_ref, f32[256,128]{1,0:T(8,128)S(1)} %get-tuple-element.21, s16[32,1152]{1,0:T(8,128)(2,1)S(1)} %collective-permute-done.5, ...), kind=kCustom, calls=%fused_computation.23 | custom fusion | bytes 675840 | tf_op jit(solution)/shard_map/compress_node/pallas_call | solution.py:140
  201.6 4.1 %collective-permute-start.6 = (s16[32,1152]{1,0:T(8,128)(2,1)S(1)}, s16[32,1152]{1,0:T(8,128)(2,1)S(1)}, u32[]{:S(2)}, u32[]{:S(2)}) collective-permute-start(s16[32,1152]{1,0:T(8,128)(2,1)S(1)} %get-tuple-element.42), channel_id=1, source_target_pairs={{0,64},{32,96},{64,0},{96,32},{128,192},{160,224},{192,128},{224,1... | collective-permute-start | bytes 221192 | tf_op jit(solution)/shard_map/ppermute | solution.py:335
  205.6 1.9 collective-permute-done.6
  207.6 6.3 %compress_node.6 = (f32[5,128,256]{2,1,0:T(8,128)S(1)}, f32[256,128]{1,0:T(8,128)S(1)}, s16[32,1152]{1,0:T(8,128)(2,1)S(1)}) fusion(f32[5,128,256]{2,1,0:T(8,128)S(1)} %get-tuple-element.39, s32[5,2]{1,0:T(8,128)S(1)} %copy.14.table_ref, f32[256,128]{1,0:T(8,128)S(1)} %get-tuple-element.40, s16[32,1152]{1,0:T(8,128)(2,1)S(1)} %collective-permute-done.6, ...), kind=kCustom, calls=%fused_computation.22 | custom fusion | bytes 675840 | tf_op jit(solution)/shard_map/compress_node/pallas_call | solution.py:140
  213.9 6.8 %collective-permute-start.7 = (s16[32,1152]{1,0:T(8,128)(2,1)S(1)}, s16[32,1152]{1,0:T(8,128)(2,1)S(1)}, u32[]{:S(2)}, u32[]{:S(2)}) collective-permute-start(s16[32,1152]{1,0:T(8,128)(2,1)S(1)} %get-tuple-element.36), channel_id=1, source_target_pairs={{0,128},{32,160},{64,192},{96,224},{128,0},{160,32},{192,64},{224,... | collective-permute-start | bytes 221192 | tf_op jit(solution)/shard_map/ppermute | solution.py:335
  220.7 2.1 collective-permute-done.7
  222.9 6.2 %compress_node.5 = (f32[5,128,256]{2,1,0:T(8,128)S(1)}, f32[256,128]{1,0:T(8,128)S(1)}) fusion(f32[5,128,256]{2,1,0:T(8,128)S(1)} %get-tuple-element.33, s32[5,2]{1,0:T(8,128)S(1)} %copy.14.table_ref, f32[256,128]{1,0:T(8,128)S(1)} %get-tuple-element.34, s16[32,1152]{1,0:T(8,128)(2,1)S(1)} %collective-permute-done.7, f32[256,128]{1,0:T(8,128)S(1)} %get-tuple-element.47), kind=kCustom, calls=%fused_computation.21 | custom fusion | bytes 602112 | tf_op jit(solution)/shard_map/compress_node/pallas_call | solution.py:140
  229.1 12.0 %collective-permute-start.8 = (f32[16,128]{1,0:T(8,128)S(1)}, f32[16,128]{1,0:T(8,128)S(1)}, u32[]{:S(2)}, u32[]{:S(2)}) collective-permute-start(f32[16,128]{1,0:T(8,128)S(1)} %constant_dynamic-slice_fusion), channel_id=1, source_target_pairs={{0,480},{32,448},{64,416},{96,384},{128,352},{160,320},{192,288},{... | collective-permute-start | bytes 24584 | tf_op jit(solution)/shard_map/ppermute | solution.py:338
  241.1 1.0 collective-permute-done.8
  242.1 0.6 pad_maximum_fusion
  (18 shorter events, 0.1 us)
Async XLA Ops:
  0.6 1.5 copy-start
  5.1 11.8 %collective-permute-start = (f32[256,1024]{1,0:T(8,128)S(1)}, f32[256,1024]{1,0:T(8,128)S(1)}, u32[]{:S(2)}, u32[]{:S(2)}) collective-permute-start(f32[256,1024]{1,0:T(8,128)S(1)} %fusion.27), channel_id=1, source_target_pairs={{0,1},{1,0},{2,3},{3,2},{4,5},{5,4},{6,7},{7,6},{8,9},{9,8},{10,11... | collective-permute-start | bytes 3145736 | tf_op jit(solution)/shard_map/ppermute | solution.py:151
  45.7 7.0 %collective-permute-start.1 = (bf16[256,1024]{1,0:T(8,128)(2,1)S(1)}, bf16[256,1024]{1,0:T(8,128)(2,1)S(1)}, u32[]{:S(2)}, u32[]{:S(2)}) collective-permute-start(bf16[256,1024]{1,0:T(8,128)(2,1)S(1)} %bitcast.42), channel_id=1, source_target_pairs={{0,1},{1,0},{2,3},{3,2},{4,5},{5,4},{6,7},{7,6},{8,9},{9,8},{10,11... | collective-permute-start | bytes 1572872 | tf_op jit(solution)/shard_map/ppermute | solution.py:151
  52.7 73.8 %copy-start.1 = (bf16[2048,1024]{1,0:T(8,128)(2,1)S(1)}, bf16[2048,1024]{1,0:T(8,128)(2,1)}, u32[]{:S(2)}) copy-start(bf16[2048,1024]{1,0:T(8,128)(2,1)} %param.5) | copy-start | bytes 12582916
  56.4 13.5 %collective-permute-start.2 = (s16[8,8,2176]{2,1,0:T(8,128)(2,1)S(1)}, s16[8,8,2176]{2,1,0:T(8,128)(2,1)S(1)}, u32[]{:S(2)}, u32[]{:S(2)}) collective-permute-start(s16[8,8,2176]{2,1,0:T(8,128)(2,1)S(1)} %give.1), channel_id=1, source_target_pairs={{0,32},{1,481},{32,0},{33,65},{64,96},{65,33},{96,64},{97,129},{12... | collective-permute-start | bytes 835592 | tf_op jit(solution)/shard_map/ppermute | solution.py:312
  128.0 32.8 %copy-start.4 = (s32[6]{0:T(128)S(1)}, s32[6]{0:T(128)}, u32[]{:S(2)}) copy-start(s32[6]{0:T(128)} %param.9) | copy-start | bytes 76
  128.0 32.9 %copy-start.2 = (f32[6,256,128]{2,1,0:T(8,128)S(1)}, f32[6,256,128]{2,1,0:T(8,128)}, u32[]{:S(2)}) copy-start(f32[6,256,128]{2,1,0:T(8,128)} %param.8) | copy-start | bytes 2359300
  128.0 11.3 %collective-permute-start.3 = (f32[256,1024]{1,0:T(8,128)S(1)}, f32[256,1024]{1,0:T(8,128)S(1)}, u32[]{:S(2)}, u32[]{:S(2)}) collective-permute-start(f32[256,1024]{1,0:T(8,128)S(1)} %fusion.36), channel_id=1, source_target_pairs={{0,1},{1,0},{2,3},{3,2},{4,5},{5,4},{6,7},{7,6},{8,9},{9,8},{10,11... | collective-permute-start | bytes 3145736 | tf_op jit(solution)/shard_map/ppermute | solution.py:151
  140.7 14.9 %all-to-all-start.4 = ((s16[16,8,2176]{2,1,0:T(8,128)(2,1)}), s16[16,8,2176]{2,1,0:T(8,128)(2,1)S(1)}, u32[]{:S(2)}, u32[]{:S(2)}) async-start(s16[16,8,2176]{2,1,0:T(8,128)(2,1)} %encode.3), calls=%async_computation.4 | async-start | bytes 1114112 | tf_op jit(solution)/shard_map/all_to_all | solution.py:155
  157.0 14.1 %all-to-all-start.5 = ((s16[16,8,2176]{2,1,0:T(8,128)(2,1)}), s16[16,8,2176]{2,1,0:T(8,128)(2,1)S(1)}, u32[]{:S(2)}, u32[]{:S(2)}) async-start(s16[16,8,2176]{2,1,0:T(8,128)(2,1)} %merge.5), calls=%async_computation.5 | async-start | bytes 1114112 | tf_op jit(solution)/shard_map/all_to_all | solution.py:155
  178.7 5.1 %collective-permute-start.4 = (s16[32,1152]{1,0:T(8,128)(2,1)S(1)}, s16[32,1152]{1,0:T(8,128)(2,1)S(1)}, u32[]{:S(2)}, u32[]{:S(2)}) collective-permute-start(s16[32,1152]{1,0:T(8,128)(2,1)S(1)} %get-tuple-element.19), channel_id=1, source_target_pairs={{0,1},{1,0},{2,3},{3,2},{4,5},{5,4},{6,7},{7,6},{8,9},{9,8},{10,11... | collective-permute-start | bytes 221192 | tf_op jit(solution)/shard_map/ppermute | solution.py:151
  190.2 5.1 %collective-permute-start.5 = (s16[32,1152]{1,0:T(8,128)(2,1)S(1)}, s16[32,1152]{1,0:T(8,128)(2,1)S(1)}, u32[]{:S(2)}, u32[]{:S(2)}) collective-permute-start(s16[32,1152]{1,0:T(8,128)(2,1)S(1)} %get-tuple-element.22), channel_id=1, source_target_pairs={{0,32},{32,0},{64,96},{96,64},{128,160},{160,128},{192,224},{224,1... | collective-permute-start | bytes 221192 | tf_op jit(solution)/shard_map/ppermute | solution.py:335
  201.6 6.0 %collective-permute-start.6 = (s16[32,1152]{1,0:T(8,128)(2,1)S(1)}, s16[32,1152]{1,0:T(8,128)(2,1)S(1)}, u32[]{:S(2)}, u32[]{:S(2)}) collective-permute-start(s16[32,1152]{1,0:T(8,128)(2,1)S(1)} %get-tuple-element.42), channel_id=1, source_target_pairs={{0,64},{32,96},{64,0},{96,32},{128,192},{160,224},{192,128},{224,1... | collective-permute-start | bytes 221192 | tf_op jit(solution)/shard_map/ppermute | solution.py:335
  213.9 9.0 %collective-permute-start.7 = (s16[32,1152]{1,0:T(8,128)(2,1)S(1)}, s16[32,1152]{1,0:T(8,128)(2,1)S(1)}, u32[]{:S(2)}, u32[]{:S(2)}) collective-permute-start(s16[32,1152]{1,0:T(8,128)(2,1)S(1)} %get-tuple-element.36), channel_id=1, source_target_pairs={{0,128},{32,160},{64,192},{96,224},{128,0},{160,32},{192,64},{224,... | collective-permute-start | bytes 221192 | tf_op jit(solution)/shard_map/ppermute | solution.py:335
  229.1 13.0 %collective-permute-start.8 = (f32[16,128]{1,0:T(8,128)S(1)}, f32[16,128]{1,0:T(8,128)S(1)}, u32[]{:S(2)}, u32[]{:S(2)}) collective-permute-start(f32[16,128]{1,0:T(8,128)S(1)} %constant_dynamic-slice_fusion), channel_id=1, source_target_pairs={{0,480},{32,448},{64,416},{96,384},{128,352},{160,320},{192,288},{... | collective-permute-start | bytes 24584 | tf_op jit(solution)/shard_map/ppermute | solution.py:338
  241.0 1.6 copy-start.3
